TPU v7x, 256 devices: a whole 4x4x8 slice. The times are simulated.
256 devices in a mesh: img: 8 (over x, core), vol: 32 (over y, z).
Axes of the slice: x: 4, y: 4, z: 8, core: 2. Of those that a mesh axis runs over, the one named last changes fastest.
Arguments:
- images: bfloat16 [2, 3072, 256, 128], P(None, 'img', 'vol'), may hold values from -6 to 6
- defocus: float32 [3072], P('img'), may hold values from 20 to 200
- candidates: int32 [3072, 8], P('img'), may hold values from 0 to 63, all different within a row
- counts: int32 [3072], P('img'), may hold values from 1 to 8
- noise_weight: float32 [256, 128], P('vol'), may hold values from 0.002 to 0.02
- volume: float32 [2, 256, 256, 128], P(None, 'vol'), may hold values from -6 to 6
- row_plane: int32 [64, 256], replicated, may hold values from 0 to 255
- row_line: int32 [64, 256], replicated, may hold values from 0 to 254
- row_weight: float32 [64, 256], replicated, may hold values from 0 to 1
- regularizer: float32 [256, 256, 128], P('vol', 'img'), may hold values from 0.05 to 0.5
Outputs:
- new_volume: float32 [2, 256, 256, 128], P(None, 'vol', 'img')
Inputs may be any that keep to these rules, and one draw needn't show every extreme that they name: The entries of one row of candidates are distinct; only the first counts entries are used.
All inputs are finite; a program needn't handle non-finite values.
Results may differ from a plain program's by a relative error of at most 0.0066.
Values may be sent and summed in bfloat16 or wider, within the bound.
A program may use at most 128 MiB of HBM per device.

v0:
```python
import math

import jax
import jax.numpy as jnp
from jax import lax
from jax.sharding import PartitionSpec as P

ROWS = 256
COLS = 128
K = 64
TRANS = 4


AMPLITUDE = 0.1


def contrast_of(defocus, row_freq, col_freq):
    radius_sq = row_freq[:, None] * row_freq[:, None] + col_freq[None, :] * col_freq[None, :]
    angle = defocus[:, None, None] * radius_sq[None]
    return -(math.sqrt(1.0 - AMPLITUDE * AMPLITUDE) * jnp.sin(angle) + AMPLITUDE * jnp.cos(angle))


def shift_phases(row_freq, col_freq, number):
    shift_ids = jnp.arange(number)
    shift_x = (shift_ids % 2).astype(jnp.float32) - 0.5
    shift_y = (shift_ids // 2).astype(jnp.float32) - 0.5
    angle = (
        -2.0
        * math.pi
        * (
            shift_x[:, None, None] * col_freq[None, None, :]
            + shift_y[:, None, None] * row_freq[None, :, None]
        )
    )
    return (jnp.cos(angle), jnp.sin(angle))


def make_references(slices, cosine, sine):
    real_part = slices[0].astype(jnp.float32)
    imag_part = slices[1].astype(jnp.float32)
    shift_re = cosine[:, None] * real_part[None] - sine[:, None] * imag_part[None]
    shift_im = sine[:, None] * real_part[None] + cosine[:, None] * imag_part[None]
    shifted = jnp.stack([shift_re, shift_im], axis=2).astype(jnp.bfloat16)
    power = (real_part * real_part + imag_part * imag_part).astype(jnp.bfloat16)
    return (shifted, power)


def posterior_of(logits, candidates, counts):
    orientation = jnp.arange(logits.shape[2])
    in_list = jnp.arange(candidates.shape[1])[None, :] < counts[:, None]
    listed = jnp.any(
        (candidates[:, :, None] == orientation[None, None, :]) & in_list[:, :, None], axis=1
    )
    allowed = listed[:, None, :]
    masked = jnp.where(allowed, logits, -1e30)
    highest = jnp.max(masked, axis=(1, 2), keepdims=True)
    exponent = jnp.where(allowed, jnp.exp(masked - highest), 0.0)
    return (exponent / jnp.sum(exponent, axis=(1, 2), keepdims=True)).astype(jnp.bfloat16)


def extract_rows(volume, plane_part, line_part, weight_part, slab_id):
    planes_here = volume.shape[1]
    flat = volume.reshape(2, planes_here * ROWS, COLS)
    local_plane = plane_part - slab_id * planes_here
    owned = (local_plane >= 0) & (local_plane < planes_here)
    line_index = jnp.clip(local_plane, 0, planes_here - 1) * ROWS + line_part
    lower = jnp.take(flat, line_index, axis=1)
    upper = jnp.take(flat, line_index + 1, axis=1)
    weight = weight_part[None, :, :, None]
    values = weight * lower + (1.0 - weight) * upper
    rounded = jnp.where(owned[None, :, :, None], values, 0.0).astype(jnp.bfloat16)
    return lax.optimization_barrier(rounded).astype(jnp.float32)


def insert_into(
    carry, piece, planes_all, lines_all, weights_all, slab_id, planes_here, line_first, line_count
):
    orient_count = piece.shape[0]
    number = piece.shape[1]
    local_plane = planes_all - slab_id * planes_here
    local_line = lines_all - line_first
    in_slab = (local_plane >= 0) & (local_plane < planes_here)
    lower_ok = in_slab & (local_line >= 0) & (local_line < line_count)
    upper_ok = in_slab & (local_line + 1 >= 0) & (local_line + 1 < line_count)
    dump_row = planes_here * line_count
    lower_index = jnp.where(lower_ok, local_plane * line_count + local_line, dump_row).reshape(-1)
    upper_index = jnp.where(upper_ok, local_plane * line_count + local_line + 1, dump_row).reshape(
        -1
    )
    values = piece.reshape(orient_count * number, 3 * COLS)
    weight = weights_all.reshape(-1, 1)
    carry = carry.at[lower_index].add(weight * values)
    return carry.at[upper_index].add((1.0 - weight) * values)


def body(
    images,
    defocus,
    candidates,
    counts,
    noise_weight,
    volume,
    row_plane,
    row_line,
    row_weight,
    regularizer,
):
    local_rows = noise_weight.shape[0]
    slab_id = lax.axis_index("vol")
    global_rows = slab_id * local_rows + jnp.arange(local_rows)
    row_freq = (global_rows.astype(jnp.float32) - ROWS // 2) / ROWS
    col_freq = jnp.arange(COLS).astype(jnp.float32) / (2 * COLS)
    img_count = lax.axis_size("img")
    group_id = lax.axis_index("img")
    share = K // img_count
    first = group_id * share
    plane_share = lax.dynamic_slice_in_dim(row_plane, first, share, 0)
    line_share = lax.dynamic_slice_in_dim(row_line, first, share, 0)
    weight_share = lax.dynamic_slice_in_dim(row_weight, first, share, 0)
    masked = extract_rows(volume, row_plane, row_line, row_weight, slab_id)
    slices = lax.psum_scatter(masked.astype(jnp.bfloat16), "vol", scatter_dimension=2, tiled=True)
    cosine, sine = shift_phases(row_freq, col_freq, TRANS)
    shifted, power = make_references(slices, cosine, sine)
    contrast = contrast_of(defocus, row_freq, col_freq)
    weighted = ((contrast * noise_weight)[None] * images).astype(jnp.bfloat16)
    squared = (contrast * contrast * noise_weight).astype(jnp.bfloat16)
    cross = jnp.einsum("jbrc,tkjrc->btk", weighted, shifted, preferred_element_type=jnp.float32)
    quadratic = jnp.einsum("brc,krc->bk", squared, power, preferred_element_type=jnp.float32)
    partial_logits = cross - 0.5 * quadratic[:, None, :]
    logits = lax.psum(partial_logits, "vol")
    weights = posterior_of(logits, candidates, counts)
    planes_here = volume.shape[1]
    y_part = jnp.einsum("btk,jbrc->tkrjc", weights, weighted, preferred_element_type=jnp.float32)
    d_part = jnp.einsum("btk,brc->tkrc", weights, squared, preferred_element_type=jnp.float32)
    num_re = jnp.sum(
        cosine[:, None] * y_part[:, :, :, 0] + sine[:, None] * y_part[:, :, :, 1], axis=0
    )
    num_im = jnp.sum(
        cosine[:, None] * y_part[:, :, :, 1] - sine[:, None] * y_part[:, :, :, 0], axis=0
    )
    partial_value = lax.psum_scatter(
        jnp.stack([num_re, num_im, jnp.sum(d_part, axis=0)], axis=2),
        "img",
        scatter_dimension=0,
        tiled=True,
    )
    initial = jnp.zeros((planes_here * ROWS + 1, 3 * COLS), jnp.float32)
    inserted = insert_into(
        initial,
        lax.all_gather(partial_value, "vol", axis=1, tiled=True),
        plane_share,
        line_share,
        weight_share,
        slab_id,
        planes_here,
        0,
        ROWS,
    )
    slab = inserted[: planes_here * ROWS].reshape(planes_here, ROWS, 3, COLS)
    summed = lax.psum_scatter(slab, "img", scatter_dimension=1, tiled=True)
    denom = summed[:, :, 2] + regularizer
    return jnp.stack([summed[:, :, 0] / denom, summed[:, :, 1] / denom], axis=0)


def solution(mesh):
    return jax.shard_map(
        body,
        mesh=mesh,
        in_specs=(
            P(None, "img", "vol", None),
            P("img"),
            P("img", None),
            P("img"),
            P("vol", None),
            P(None, "vol", None, None),
            P(),
            P(),
            P(),
            P("vol", "img", None),
        ),
        out_specs=P(None, "vol", "img", None),
        check_vma=False,
    )
```

profile of v0, /device:TPU:1, one launch (start us, length us, event | category | flops | bytes accessed | tf_op | source)
XLA Modules:
  0.0 920.6 jit_solution(6707213420497245051)
XLA Ops:
  7.6 3.2 copy.81
  10.8 112.6 %gather_fusion = f32[16384,2,128]{2,1,0:T(2,128)} fusion(f32[2,2048,128]{2,0,1:T(2,128)S(1)} %bitcast.135, s32[16384]{0:T(1024)S(1)} %broadcast_clamp_fusion.1), kind=kCustom, calls=%fused_computation.clone | custom fusion | bytes 33619968 | tf_op jit(solution)/shard_map/jit(_take)/gather | solution.py:67
  123.4 12.6 %copy.82 = f32[16384,2,128]{2,0,1:T(8,128)} copy(f32[16384,2,128]{2,1,0:T(2,128)} %gather_fusion) | data formatting | bytes 33554432 | tf_op jit(solution)/shard_map/jit(_take)/gather | solution.py:67
  136.1 112.6 %gather_fusion.1 = f32[16384,2,128]{2,1,0:T(2,128)} fusion(f32[2,2048,128]{2,0,1:T(2,128)S(1)} %bitcast.136, s32[16384]{0:T(1024)S(1)} %broadcast_clamp_fusion), kind=kCustom, calls=%fused_computation.1.clone | custom fusion | bytes 33619968 | tf_op jit(solution)/shard_map/jit(_take)/gather | solution.py:68
  248.6 8.1 copy.83
  256.8 16.6 %fusion.2 = bf16[2,64,256,128]{3,2,1,0:T(8,128)(2,1)} fusion(f32[64,256,2,128]{3,1,0,2:T(8,128)S(1)} %bitcast.138, f32[64,256,2,128]{3,1,0,2:T(8,128)} %bitcast.137, f32[64,256]{1,0:T(8,128)S(1)} %broadcast_subtract_fusion, f32[64,256]{1,0:T(8,128)S(1)} %copy-done.3, pred[64,256]{1,0:T(8,128)(4,1)S(1)} %compare_and_fusion, ...), kind=kLoop, calls=%fused_computation.7 | loop fusion | flops 29360128 | bytes 42123264 | tf_op jit(solution)/shard_map/convert_element_type | solution.py:71
  273.4 12.0 %copy.109 = bf16[2,64,256,128]{3,1,0,2:T(8,128)(2,1)} copy(bf16[2,64,256,128]{3,2,1,0:T(8,128)(2,1)} %fusion.2) | data formatting | bytes 16777216
  285.4 23.4 %copy.145 = bf16[32,8,128,128]{3,1,2,0:T(8,128)(2,1)} copy(bf16[32,8,128,128]{3,2,1,0:T(8,128)(2,1)} %bitcast.140) | data formatting | bytes 16777216
  309.5 5.7 fusion.10
  318.0 220.2 %reduce-scatter.10.cloned.1.call-done = bf16[8,16384]{1,0:T(8,128)(2,1)} async-done(((bf16[256,16384]{1,0:T(8,128)(2,1)}), bf16[8,16384]{1,0:T(8,128)(2,1)}) %reduce-scatter.10.cloned.1.call-update) | async-done | bytes 262160
  539.7 6.2 fusion.23
  549.5 141.5 %all-reduce.2.cloned.1.call-done = f32[384,4,64]{0,2,1:T(8,128)} async-done(((f32[384,4,64]{0,2,1:T(8,128)}), f32[384,4,64]{0,2,1:T(8,128)}) %all-reduce.2.cloned.1.call-update) | async-done | bytes 393232 | tf_op jit(solution)/shard_map/psum | solution.py:130
  696.3 6.1 convolution_reduce_fusion
  703.5 33.6 %reduce-scatter.6.cloned.1.call-done = f32[8,8,3,128]{3,0,1,2:T(8,128)} async-done(((f32[64,8,3,128]{3,0,1,2:T(8,128)}), f32[8,8,3,128]{3,0,1,2:T(8,128)}) %reduce-scatter.6.cloned.1.call-update) | async-done | bytes 98320 | tf_op jit(solution)/shard_map/reduce_scatter | solution.py:141
  740.5 76.7 %all-gather.2.cloned.1.call-done = f32[8,256,3,128]{3,0,2,1:T(8,128)} async-done(((f32[8,8,3,128]{3,0,2,1:T(8,128)}), f32[8,256,3,128]{3,0,2,1:T(8,128)}) %all-gather.2.cloned.1.call-update) | async-done | bytes 3145744 | tf_op jit(solution)/shard_map/all_gather | solution.py:150
  817.1 2.6 copy.91
  821.1 2.5 broadcast_multiply_fusion
  823.6 3.5 copy.92
  827.2 2.4 copy.93
  829.6 16.0 %scatter_custom_fusion = f32[2049,384]{1,0:T(8,128)S(1)} fusion(s32[2048]{0:T(1024)S(1)} %bitcast.155, f32[2048,384]{1,0:T(8,128)} %copy.92, f32[]{:T(128)} %constant.33.clone.1), kind=kCustom, calls=%fused_computation.14 | custom fusion | flops 786432 | bytes 3147776 | tf_op jit(solution)/shard_map/scatter-add | solution.py:92
  845.5 16.6 %scatter_fusion = f32[2049,384]{1,0:T(8,128)S(1)} fusion(f32[2049,384]{1,0:T(8,128)S(1)} %scatter_custom_fusion, s32[2048]{0:T(1024)S(1)} %bitcast.154, f32[2048,384]{1,0:T(8,128)} %copy.93), kind=kCustom, calls=%fused_computation.3 | custom fusion | flops 786432 | bytes 9445376 | tf_op jit(solution)/shard_map/scatter-add | solution.py:93
  864.0 5.7 reshape.355
  869.8 5.7 copy.95
  875.5 36.2 %reduce-scatter.8.cloned.1.call-done = f32[8,32,3,128]{3,0,2,1:T(8,128)} async-done(((f32[8,256,3,128]{3,0,2,1:T(8,128)}), f32[8,32,3,128]{3,0,2,1:T(8,128)}) %reduce-scatter.8.cloned.1.call-update) | async-done | bytes 393232 | tf_op jit(solution)/shard_map/reduce_scatter | solution.py:160
  (80 shorter events, 24.4 us)
Async XLA Ops:
  6.5 531.7 %reduce-scatter.10.cloned.1.call-start = ((), (), s32[]{:S(2)}) async-start(), calls=%async_computation.7 | async-start | bytes 8650752
  248.6 8.1 copy-start.3
  308.8 0.7 copy-start.6
  308.8 0.7 copy-start.7
  308.8 382.1 %all-reduce.2.cloned.1.call-start = ((), (), s32[]{:S(2)}) async-start(), calls=%async_computation.3 | async-start | bytes 786432 | tf_op jit(solution)/shard_map/psum | solution.py:130
  309.5 6.8 copy-start.8
  309.5 7.0 copy-start
  539.7 6.5 copy-start.2
  546.2 1.6 copy-start.5
  547.8 189.2 %reduce-scatter.6.cloned.1.call-start = ((), (), s32[]{:S(2)}) async-start(), calls=%async_computation.4 | async-start | bytes 884736 | tf_op jit(solution)/shard_map/reduce_scatter | solution.py:141
  695.3 1.0 copy-start.1
  703.4 113.7 %all-gather.2.cloned.1.call-start = ((), (), s32[]{:S(2)}) async-start(), calls=%async_computation.5 | async-start | bytes 3244032 | tf_op jit(solution)/shard_map/all_gather | solution.py:150
  738.6 173.1 %reduce-scatter.8.cloned.1.call-start = ((), (), s32[]{:S(2)}) async-start(), calls=%async_computation.6 | async-start | bytes 3538944 | tf_op jit(solution)/shard_map/reduce_scatter | solution.py:160
  875.5 36.2 %copy-start.4 = (f32[8,32,128]{2,1,0:T(8,128)S(1)}, f32[8,32,128]{2,1,0:T(8,128)}, u32[]{:S(2)}) copy-start(f32[8,32,128]{2,1,0:T(8,128)} %param.21) | copy-start | bytes 393220
Sparse Core Ops, SparseCore 0:
  308.9 229.2 reduce-scatter.9
  547.9 142.9 all-reduce.1
  703.5 33.4 reduce-scatter.5
  739.8 77.2 all-gather.1
  875.6 36.0 reduce-scatter.7
where the time goes:
time: 927 us; the launch traced here: 921 us
  waiting for transfers between devices  508 us (55%)
  local copies, waits for them, and re-layouts  312 us (34%)
  other arithmetic  69.4 us (7%)
  matrix products  16.1 us (2%)
  between operations  14 us (2%)
    unnamed x6, waiting for transfers between devices  220 us
    psum x1, waiting for transfers between devices, body(): logits = lax.psum(partial_logits, 'vol')  141 us
    gather x2, local copies, waits for them, and re-layouts, extract_rows(): lower = jnp.take(flat, line_index, axis=1)  125 us
    gather x2, local copies, waits for them, and re-layouts, extract_rows(): upper = jnp.take(flat, line_index + 1, axis=1)  121 us
    all_gather x1, waiting for transfers between devices, body(): lax.all_gather(partial_value, 'vol', axis=1, tiled=True)  76.7 us
    unnamed x29, local copies, waits for them, and re-layouts  42 us
    reduce_scatter x1, waiting for transfers between devices, body(): summed = lax.psum_scatter(slab, 'img', scatter_dimension=1, tiled=True)  36.2 us
    reduce_scatter x1, waiting for transfers between devices, body(): lax.psum_scatter(jnp.stack([num_re, num_im, jnp.sum(d_part, axis=0)], axi...  33.6 us
  transfers between devices with their start and end apart: 5, of which 5 were waited for; matrix products, arithmetic and copies ran while one was open for 1% of the time, Pallas kernels for 0%

commit v1 on v0

--- a/solution.py
+++ b/solution.py
@@ -45,13 +45,8 @@
     return (shifted, power)
 
 
-def posterior_of(logits, candidates, counts):
-    orientation = jnp.arange(logits.shape[2])
-    in_list = jnp.arange(candidates.shape[1])[None, :] < counts[:, None]
-    listed = jnp.any(
-        (candidates[:, :, None] == orientation[None, None, :]) & in_list[:, :, None], axis=1
-    )
-    allowed = listed[:, None, :]
+def posterior_of(logits, counts):
+    allowed = (jnp.arange(logits.shape[2])[None, :] < counts[:, None])[:, None, :]
     masked = jnp.where(allowed, logits, -1e30)
     highest = jnp.max(masked, axis=(1, 2), keepdims=True)
     exponent = jnp.where(allowed, jnp.exp(masked - highest), 0.0)
@@ -117,8 +112,9 @@
     plane_share = lax.dynamic_slice_in_dim(row_plane, first, share, 0)
     line_share = lax.dynamic_slice_in_dim(row_line, first, share, 0)
     weight_share = lax.dynamic_slice_in_dim(row_weight, first, share, 0)
-    masked = extract_rows(volume, row_plane, row_line, row_weight, slab_id)
-    slices = lax.psum_scatter(masked.astype(jnp.bfloat16), "vol", scatter_dimension=2, tiled=True)
+    masked = extract_rows(volume, plane_share, line_share, weight_share, slab_id)
+    own_rows = lax.psum_scatter(masked.astype(jnp.bfloat16), "vol", scatter_dimension=2, tiled=True)
+    slices = lax.all_gather(own_rows, "img", axis=1, tiled=True)
     cosine, sine = shift_phases(row_freq, col_freq, TRANS)
     shifted, power = make_references(slices, cosine, sine)
     contrast = contrast_of(defocus, row_freq, col_freq)
@@ -127,8 +123,17 @@
     cross = jnp.einsum("jbrc,tkjrc->btk", weighted, shifted, preferred_element_type=jnp.float32)
     quadratic = jnp.einsum("brc,krc->bk", squared, power, preferred_element_type=jnp.float32)
     partial_logits = cross - 0.5 * quadratic[:, None, :]
-    logits = lax.psum(partial_logits, "vol")
-    weights = posterior_of(logits, candidates, counts)
+    orientation = jnp.arange(K, dtype=jnp.int32)
+    pick = candidates[:, :, None] == orientation[None, None, :]
+    chosen = jnp.sum(
+        jnp.where(pick[:, None, :, :], partial_logits[:, :, None, :], 0.0), axis=3
+    )
+    logits = lax.psum(chosen, "vol")
+    listed = posterior_of(logits, counts)
+    weights = jnp.sum(
+        jnp.where(pick[:, None, :, :], listed[:, :, :, None], jnp.zeros((), jnp.bfloat16)),
+        axis=2,
+    )
     planes_here = volume.shape[1]
     y_part = jnp.einsum("btk,jbrc->tkrjc", weights, weighted, preferred_element_type=jnp.float32)
     d_part = jnp.einsum("btk,brc->tkrc", weights, squared, preferred_element_type=jnp.float32)

time: 927 us -> 653 us (0.70)
  local copies, waits for them, and re-layouts: 312 us -> 65.7 us
  waiting for transfers between devices: 508 us -> 370 us
  blocking collectives: 0 us -> 133 us
  other arithmetic: 69.4 us -> 51 us
    psum x1 -> x0, waiting for transfers between devices: 141 us -> none  [body(): logits = lax.psum(partial_logits, 'vol')]
    psum x0 -> x1, blocking collectives: none -> 113 us  [body(): logits = lax.psum(chosen, 'vol')]
    gather x2, local copies, waits for them, and re-layouts: 125 us -> 17.5 us  [extract_rows(): lower = jnp.take(flat, line_index, axis=1)]
    gather x2, local copies, waits for them, and re-layouts: 121 us -> 16.3 us  [extract_rows(): upper = jnp.take(flat, line_index + 1, axis=1)]
    unnamed x29 -> x25, local copies, waits for them, and re-layouts: 42 us -> 7.42 us
    all_gather x0 -> x1, blocking collectives: none -> 19.7 us  [body(): slices = lax.all_gather(own_rows, 'img', axis=1, tiled=True)]
    reduce_scatter x1, waiting for transfers between devices: 33.6 us -> 51.7 us  [body(): lax.psum_scatter(jnp.stack([num_re, num_im, jnp.sum(d_part, axis=0)], axi...]
    unnamed x6 -> x5, waiting for transfers between devices: 220 us -> 204 us
  transfers between devices with their start and end apart: 5 -> 4, of which waited for: 5 -> 4; matrix products, arithmetic and copies ran while one was open for 1% -> 1% of each run, Pallas kernels for 0% -> 0%
where the time goes in v1:
time: 653 us; the launch traced here: 647 us
  waiting for transfers between devices  370 us (57%)
  blocking collectives  133 us (20%)
  local copies, waits for them, and re-layouts  65.7 us (10%)
  other arithmetic  51 us (8%)
  between operations  13.8 us (2%)
  matrix products  13.5 us (2%)
    unnamed x5, waiting for transfers between devices  204 us
    psum x1, blocking collectives, body(): logits = lax.psum(chosen, 'vol')  113 us
    all_gather x1, waiting for transfers between devices, body(): lax.all_gather(partial_value, 'vol', axis=1, tiled=True)  77.5 us
    reduce_scatter x1, waiting for transfers between devices, body(): lax.psum_scatter(jnp.stack([num_re, num_im, jnp.sum(d_part, axis=0)], axi...  51.7 us
    reduce_scatter x1, waiting for transfers between devices, body(): summed = lax.psum_scatter(slab, 'img', scatter_dimension=1, tiled=True)  36.1 us
    all_gather x1, blocking collectives, body(): slices = lax.all_gather(own_rows, 'img', axis=1, tiled=True)  19.7 us
    gather x2, local copies, waits for them, and re-layouts, extract_rows(): lower = jnp.take(flat, line_index, axis=1)  17.5 us
    scatter-add x1, other arithmetic, insert_into(): return carry.at[upper_index].add((1.0 - weight) * values)  16.6 us
  transfers between devices with their start and end apart: 4, of which 4 were waited for; matrix products, arithmetic and copies ran while one was open for 1% of the time, Pallas kernels for 0%

profile of v1, /device:TPU:1, one launch (start us, length us, event | category | flops | bytes accessed | tf_op | source)
XLA Modules:
  0.0 646.7 jit_solution(17076826061948792427)
XLA Ops:
  8.0 3.2 copy.85
  11.3 14.4 %gather_fusion = f32[2048,2,128]{2,1,0:T(2,128)} fusion(f32[2,2048,128]{2,0,1:T(2,128)S(1)} %bitcast.137, s32[2048]{0:T(1024)S(1)} %broadcast_clamp_fusion.1), kind=kCustom, calls=%fused_computation.clone | custom fusion | bytes 4202496 | tf_op jit(solution)/shard_map/jit(_take)/gather | solution.py:62
  25.7 3.1 copy.86
  28.8 14.4 %gather_fusion.1 = f32[2048,2,128]{2,1,0:T(2,128)} fusion(f32[2,2048,128]{2,0,1:T(2,128)S(1)} %bitcast.138, s32[2048]{0:T(1024)S(1)} %broadcast_clamp_fusion), kind=kCustom, calls=%fused_computation.1.clone | custom fusion | bytes 4202496 | tf_op jit(solution)/shard_map/jit(_take)/gather | solution.py:63
  43.2 1.9 copy.87
  45.8 1.7 fusion.2
  50.0 5.7 fusion.10
  57.8 204.1 %reduce-scatter.10.cloned.1.call-done = bf16[8,2048]{1,0:T(8,128)(2,1)} async-done(((bf16[256,2048]{1,0:T(8,128)(2,1)}), bf16[8,2048]{1,0:T(8,128)(2,1)}) %reduce-scatter.10.cloned.1.call-update) | async-done | bytes 32784
  262.7 19.7 %all_gather.6 = bf16[2,64,8,128]{3,2,1,0:T(8,128)(2,1)S(1)} all-gather(bf16[2,8,8,128]{3,2,1,0:T(8,128)(2,1)S(1)} %copy.114), channel_id=1, replica_groups=mesh['img'=8,'vol'=32] {'img'}, dimensions={1}, use_global_device_ids=true | all-gather | bytes 294912 | tf_op jit(solution)/shard_map/all_gather | solution.py:117
  282.6 6.0 fusion.23
  290.0 112.9 %psum.7 = f32[384,4,8]{0,2,1:T(8,128)S(1)} all-reduce(f32[384,4,8]{0,2,1:T(8,128)S(1)} %select_reduce_fusion), channel_id=1, replica_groups=mesh['img'=8,'vol'=32] {'vol'}, use_global_device_ids=true, to_apply=%region_2.4 | all-reduce | flops 12288 | bytes 98304 | tf_op jit(solution)/shard_map/psum | solution.py:131
  403.4 6.0 convolution_reduce_fusion
  411.6 51.7 %reduce-scatter.6.cloned.1.call-done = f32[8,8,3,128]{3,0,1,2:T(8,128)} async-done(((f32[64,8,3,128]{3,0,1,2:T(8,128)}), f32[8,8,3,128]{3,0,1,2:T(8,128)}) %reduce-scatter.6.cloned.1.call-update) | async-done | bytes 98320 | tf_op jit(solution)/shard_map/reduce_scatter | solution.py:146
  465.9 77.5 %all-gather.2.cloned.1.call-done = f32[8,256,3,128]{3,0,2,1:T(8,128)} async-done(((f32[8,8,3,128]{3,0,2,1:T(8,128)}), f32[8,256,3,128]{3,0,2,1:T(8,128)}) %all-gather.2.cloned.1.call-update) | async-done | bytes 3145744 | tf_op jit(solution)/shard_map/all_gather | solution.py:155
  543.4 2.6 copy.95
  547.5 2.5 broadcast_multiply_fusion
  549.9 3.5 copy.96
  553.5 2.4 copy.97
  555.9 16.0 %scatter_custom_fusion = f32[2049,384]{1,0:T(8,128)S(1)} fusion(s32[2048]{0:T(1024)S(1)} %bitcast.158, f32[2048,384]{1,0:T(8,128)} %copy.96, f32[]{:T(128)} %constant.33.clone.1), kind=kCustom, calls=%fused_computation.14 | custom fusion | flops 786432 | bytes 3147776 | tf_op jit(solution)/shard_map/scatter-add | solution.py:87
  571.9 16.6 %scatter_fusion = f32[2049,384]{1,0:T(8,128)S(1)} fusion(f32[2049,384]{1,0:T(8,128)S(1)} %scatter_custom_fusion, s32[2048]{0:T(1024)S(1)} %bitcast.157, f32[2048,384]{1,0:T(8,128)} %copy.97), kind=kCustom, calls=%fused_computation.3 | custom fusion | flops 786432 | bytes 9445376 | tf_op jit(solution)/shard_map/scatter-add | solution.py:88
  588.5 1.9 slice.42
  590.4 5.7 reshape.355
  596.1 5.7 copy.99
  601.8 36.1 %reduce-scatter.8.cloned.1.call-done = f32[8,32,3,128]{3,0,2,1:T(8,128)} async-done(((f32[8,256,3,128]{3,0,2,1:T(8,128)}), f32[8,32,3,128]{3,0,2,1:T(8,128)}) %reduce-scatter.8.cloned.1.call-update) | async-done | bytes 393232 | tf_op jit(solution)/shard_map/reduce_scatter | solution.py:165
  (78 shorter events, 17.5 us)
Async XLA Ops:
  6.5 255.4 %reduce-scatter.10.cloned.1.call-start = ((), (), s32[]{:S(2)}) async-start(), calls=%async_computation.6 | async-start | bytes 1081344
  43.2 2.6 copy-start
  48.2 1.8 copy-start.4
  48.2 1.8 copy-start.5
  49.5 413.8 %reduce-scatter.6.cloned.1.call-start = ((), (), s32[]{:S(2)}) async-start(), calls=%async_computation.3 | async-start | bytes 884736 | tf_op jit(solution)/shard_map/reduce_scatter | solution.py:146
  50.0 7.0 %copy-start.6 = (s32[384]{0:T(512)S(1)}, s32[384]{0:T(512)}, u32[]{:S(2)}) copy-start(s32[384]{0:T(512)} %param.15) | copy-start | bytes 4612
  50.0 7.1 %copy-start.3 = (s32[384,8]{0,1:T(8,128)S(1)}, s32[384,8]{0,1:T(8,128)}, u32[]{:S(2)}) copy-start(s32[384,8]{0,1:T(8,128)} %param.14) | copy-start | bytes 36868
  55.7 1.4 copy-start.1
  411.5 131.9 %all-gather.2.cloned.1.call-start = ((), (), s32[]{:S(2)}) async-start(), calls=%async_computation.4 | async-start | bytes 3244032 | tf_op jit(solution)/shard_map/all_gather | solution.py:155
  464.8 173.1 %reduce-scatter.8.cloned.1.call-start = ((), (), s32[]{:S(2)}) async-start(), calls=%async_computation.5 | async-start | bytes 3538944 | tf_op jit(solution)/shard_map/reduce_scatter | solution.py:165
  601.8 36.2 %copy-start.2 = (f32[8,32,128]{2,1,0:T(8,128)S(1)}, f32[8,32,128]{2,1,0:T(8,128)}, u32[]{:S(2)}) copy-start(f32[8,32,128]{2,1,0:T(8,128)} %param.21) | copy-start | bytes 393220
Sparse Core Ops, SparseCore 0:
  49.6 212.2 reduce-scatter.9
  411.6 51.5 reduce-scatter.5
  466.2 77.1 all-gather.1
  602.0 35.9 reduce-scatter.7

commit v2 on v1

--- a/solution.py
+++ b/solution.py
@@ -86,6 +86,21 @@
     weight = weights_all.reshape(-1, 1)
     carry = carry.at[lower_index].add(weight * values)
     return carry.at[upper_index].add((1.0 - weight) * values)
+
+
+def scatter_sum(x, axis_name, dim):
+    count = lax.axis_size(axis_name)
+    shape = x.shape
+    split = x.reshape(shape[:dim] + (count, shape[dim] // count) + shape[dim + 1 :])
+    received = lax.all_to_all(split, axis_name, dim, dim, tiled=True)
+    return jnp.sum(received, axis=dim)
+
+
+def gather_all(x, axis_name, dim):
+    count = lax.axis_size(axis_name)
+    copies = jnp.broadcast_to(x[None], (count,) + x.shape)
+    received = jnp.moveaxis(lax.all_to_all(copies, axis_name, 0, 0, tiled=True), 0, dim)
+    return received.reshape(x.shape[:dim] + (count * x.shape[dim],) + x.shape[dim + 1 :])
 
 
 def body(
@@ -113,8 +128,8 @@
     line_share = lax.dynamic_slice_in_dim(row_line, first, share, 0)
     weight_share = lax.dynamic_slice_in_dim(row_weight, first, share, 0)
     masked = extract_rows(volume, plane_share, line_share, weight_share, slab_id)
-    own_rows = lax.psum_scatter(masked.astype(jnp.bfloat16), "vol", scatter_dimension=2, tiled=True)
-    slices = lax.all_gather(own_rows, "img", axis=1, tiled=True)
+    own_rows = scatter_sum(masked.astype(jnp.bfloat16), "vol", 2)
+    slices = gather_all(own_rows, "img", 1)
     cosine, sine = shift_phases(row_freq, col_freq, TRANS)
     shifted, power = make_references(slices, cosine, sine)
     contrast = contrast_of(defocus, row_freq, col_freq)
@@ -128,7 +143,7 @@
     chosen = jnp.sum(
         jnp.where(pick[:, None, :, :], partial_logits[:, :, None, :], 0.0), axis=3
     )
-    logits = lax.psum(chosen, "vol")
+    logits = gather_all(scatter_sum(chosen, "vol", 0), "vol", 0)
     listed = posterior_of(logits, counts)
     weights = jnp.sum(
         jnp.where(pick[:, None, :, :], listed[:, :, :, None], jnp.zeros((), jnp.bfloat16)),
@@ -143,16 +158,13 @@
     num_im = jnp.sum(
         cosine[:, None] * y_part[:, :, :, 1] - sine[:, None] * y_part[:, :, :, 0], axis=0
     )
-    partial_value = lax.psum_scatter(
-        jnp.stack([num_re, num_im, jnp.sum(d_part, axis=0)], axis=2),
-        "img",
-        scatter_dimension=0,
-        tiled=True,
+    partial_value = scatter_sum(
+        jnp.stack([num_re, num_im, jnp.sum(d_part, axis=0)], axis=2), "img", 0
     )
     initial = jnp.zeros((planes_here * ROWS + 1, 3 * COLS), jnp.float32)
     inserted = insert_into(
         initial,
-        lax.all_gather(partial_value, "vol", axis=1, tiled=True),
+        gather_all(partial_value, "vol", 1),
         plane_share,
         line_share,
         weight_share,
@@ -162,7 +174,7 @@
         ROWS,
     )
     slab = inserted[: planes_here * ROWS].reshape(planes_here, ROWS, 3, COLS)
-    summed = lax.psum_scatter(slab, "img", scatter_dimension=1, tiled=True)
+    summed = scatter_sum(slab, "img", 1)
     denom = summed[:, :, 2] + regularizer
     return jnp.stack([summed[:, :, 0] / denom, summed[:, :, 1] / denom], axis=0)
 

time: 653 us -> 343 us (0.53)
  waiting for transfers between devices: 370 us -> 108 us
  blocking collectives: 133 us -> 63.3 us
  starting transfers between devices: 0.67 us -> 36.1 us
  between operations: 13.8 us -> 0.78 us
  local copies, waits for them, and re-layouts: 65.7 us -> 55.4 us
  other arithmetic: 51 us -> 60.3 us
    unnamed x5 -> x0, waiting for transfers between devices: 204 us -> none
    psum x1 -> x0, blocking collectives: 113 us -> none  [body(): logits = lax.psum(chosen, 'vol')]
    all_to_all x0 -> x5, waiting for transfers between devices: none -> 108 us  [the longest x3 85.2 us: gather_all(): lax.all_to_all(copies, axis_name, 0, 0, tiled=True)]
    reduce_scatter x2 -> x0, waiting for transfers between devices: 87.9 us -> none  [the longest x1 51.7 us: body(): lax.psum_scatter(jnp.stack([num_re, num_im, jnp.sum(d_part, axis=0)], axi...]
    all_gather x1 -> x0, waiting for transfers between devices: 77.5 us -> none  [body(): lax.all_gather(partial_value, 'vol', axis=1, tiled=True)]
    all_to_all x0 -> x2, blocking collectives: none -> 63.3 us  [scatter_sum(): received = lax.all_to_all(split, axis_name, dim, dim, tiled=True)]
    all_to_all x0 -> x5, starting transfers between devices: none -> 36.1 us  [the longest x3 18.9 us: gather_all(): lax.all_to_all(copies, axis_name, 0, 0, tiled=True)]
    all_gather x1 -> x0, blocking collectives: 19.7 us -> none  [body(): slices = lax.all_gather(own_rows, 'img', axis=1, tiled=True)]
  transfers between devices with their start and end apart: 4 -> 5, of which waited for: 4 -> 5; matrix products, arithmetic and copies ran while one was open for 1% -> 3% of each run, Pallas kernels for 0% -> 0%
where the time goes in v2:
time: 343 us; the launch traced here: 338 us
  waiting for transfers between devices  108 us (31%)
  blocking collectives  63.3 us (18%)
  other arithmetic  60.3 us (18%)
  local copies, waits for them, and re-layouts  55.4 us (16%)
  starting transfers between devices  36.1 us (11%)
  matrix products  13.5 us (4%)
    all_to_all x3, waiting for transfers between devices, gather_all(): lax.all_to_all(copies, axis_name, 0, 0, tiled=True)  85.2 us
    all_to_all x2, blocking collectives, scatter_sum(): received = lax.all_to_all(split, axis_name, dim, dim, tiled=True)  63.3 us
    all_to_all x2, waiting for transfers between devices, scatter_sum(): received = lax.all_to_all(split, axis_name, dim, dim, tiled=True)  23.2 us
    scatter-add x1, other arithmetic, insert_into(): return carry.at[upper_index].add((1.0 - weight) * values)  19.3 us
    all_to_all x3, starting transfers between devices, gather_all(): lax.all_to_all(copies, axis_name, 0, 0, tiled=True)  18.9 us
    scatter-add x1, other arithmetic, insert_into(): carry = carry.at[lower_index].add(weight * values)  17.6 us
    all_to_all x2, starting transfers between devices, scatter_sum(): received = lax.all_to_all(split, axis_name, dim, dim, tiled=True)  17.2 us
    gather x1, local copies, waits for them, and re-layouts, extract_rows(): upper = jnp.take(flat, line_index + 1, axis=1)  14.4 us
  transfers between devices with their start and end apart: 5, of which 5 were waited for; matrix products, arithmetic and copies ran while one was open for 3% of the time, Pallas kernels for 0%

profile of v2, /device:TPU:1, one launch (start us, length us, event | category | flops | bytes accessed | tf_op | source)
XLA Modules:
  0.0 337.8 jit_solution(2668811654256296818)
XLA Ops:
  1.5 3.2 copy.102
  4.7 14.4 %gather_fusion = f32[2048,2,128]{2,1,0:T(2,128)} fusion(f32[2,2048,128]{2,0,1:T(2,128)S(1)} %bitcast.153, s32[2048]{0:T(1024)S(1)} %broadcast_clamp_fusion.1), kind=kCustom, calls=%fused_computation.clone | custom fusion | bytes 4202496 | tf_op jit(solution)/shard_map/jit(_take)/gather | solution.py:62
  19.2 14.4 %gather_fusion.1 = f32[2048,2,128]{2,1,0:T(2,128)} fusion(f32[2,2048,128]{2,0,1:T(2,128)S(1)} %bitcast.154, s32[2048]{0:T(1024)S(1)} %broadcast_clamp_fusion), kind=kCustom, calls=%fused_computation.1.clone | custom fusion | bytes 4202496 | tf_op jit(solution)/shard_map/jit(_take)/gather | solution.py:63
  34.3 3.8 %fusion.6 = bf16[2,8,256,128]{3,2,1,0:T(8,128)(2,1)S(1)} fusion(f32[8,256,2,128]{3,2,1,0:T(2,128)} %bitcast.156, f32[8,256,2,128]{3,2,1,0:T(2,128)} %bitcast.155, f32[8,256]{1,0:T(8,128)S(1)} %get-tuple-element.12, f32[8,256]{1,0:T(8,128)S(1)} %get-tuple-element.13, pred[8,256]{1,0:T(8,128)(4,1)S(1)} %compare_and_fusion, ...), kind=kLoop, calls=%fused_computation.15 | loop fusion | flops 3670016 | bytes 5265408 | tf_op jit(solution)/shard_map/convert_element_type | solution.py:66
  38.1 2.6 copy.105
  40.7 12.5 %all-to-all-start = ((bf16[2,8,32,8,128]{4,0,3,1,2:T(2,128)(2,1)}), bf16[2,8,32,8,128]{4,0,3,1,2:T(2,128)(2,1)}, u32[]{:S(2)}, u32[]{:S(2)}) async-start(bf16[2,8,32,8,128]{4,0,3,1,2:T(2,128)(2,1)} %copy.105), calls=%async_computation | async-start | bytes 2097152 | tf_op jit(solution)/shard_map/all_to_all | solution.py:95
  53.3 5.7 %fusion.13 = f32[384,8,128]{2,0,1:T(8,128)S(1)} fusion(f32[8,128]{1,0:T(8,128)S(1)} %copy-done.5, f32[8,128]{1,0:T(8,128)S(1)} %broadcast_add_fusion, f32[384]{0:T(512)S(1)} %copy-done.6), kind=kLoop, calls=%fused_computation.26 | loop fusion | flops 2359296 | bytes 1582592 | tf_op jit(solution)/shard_map/mul | solution.py:136
  63.3 14.5 %all-to-all-done = bf16[2,8,32,8,128]{4,0,3,1,2:T(2,128)(2,1)} async-done(((bf16[2,8,32,8,128]{4,0,3,1,2:T(2,128)(2,1)}), bf16[2,8,32,8,128]{4,0,3,1,2:T(2,128)(2,1)}, u32[]{:S(2)}, u32[]{:S(2)}) %all-to-all-start) | async-done | bytes 1048608 | tf_op jit(solution)/shard_map/all_to_all | solution.py:95
  80.7 9.8 %all-to-all-start.1 = ((bf16[8,2,8,8,128]{4,2,3,1,0:T(8,128)(2,1)}), bf16[8,2,8,8,128]{4,2,3,1,0:T(8,128)(2,1)S(1)}, u32[]{:S(2)}, u32[]{:S(2)}) async-start(bf16[8,2,8,8,128]{4,2,3,1,0:T(8,128)(2,1)} %broadcast_in_dim.101), calls=%async_computation.1 | async-start | bytes 524288 | tf_op jit(solution)/shard_map/all_to_all | solution.py:102
  90.6 6.3 %all-to-all-done.1 = bf16[8,2,8,8,128]{4,2,3,1,0:T(8,128)(2,1)S(1)} async-done(((bf16[8,2,8,8,128]{4,2,3,1,0:T(8,128)(2,1)}), bf16[8,2,8,8,128]{4,2,3,1,0:T(8,128)(2,1)S(1)}, u32[]{:S(2)}, u32[]{:S(2)}) %all-to-all-start.1) | async-done | bytes 262176 | tf_op jit(solution)/shard_map/all_to_all | solution.py:102
  97.2 6.0 %fusion.28 = f32[384,64]{0,1:T(8,128)S(1)} fusion(f32[8,128]{1,0:T(8,128)S(1)} %copy-done.5, f32[8,128]{1,0:T(8,128)S(1)} %broadcast_add_fusion, f32[384]{0:T(512)S(1)} %copy-done.6, bf16[64,8,128]{2,1,0:T(8,128)(2,1)S(1)} %add_convert_fusion.1), kind=kOutput, calls=%fused_computation.40 | convolution fusion | flops 53108736 | bytes 239104 | tf_op jit(solution)/shard_map/brc,krc->bk/dot_general | solution.py:139
  107.6 4.8 %all-to-all-start.2 = ((f32[32,1,384]{2,1,0:T(1,128)}), f32[32,1,384]{2,1,0:T(1,128)S(1)}, u32[]{:S(2)}, u32[]{:S(2)}) async-start(f32[32,1,384]{2,1,0:T(1,128)} %reshape.411), calls=%async_computation.2 | async-start | bytes 98304 | tf_op jit(solution)/shard_map/all_to_all | solution.py:95
  112.4 8.8 %all-to-all-done.2 = f32[32,1,384]{2,1,0:T(1,128)S(1)} async-done(((f32[32,1,384]{2,1,0:T(1,128)}), f32[32,1,384]{2,1,0:T(1,128)S(1)}, u32[]{:S(2)}, u32[]{:S(2)}) %all-to-all-start.2) | async-done | bytes 49184 | tf_op jit(solution)/shard_map/all_to_all | solution.py:95
  124.2 4.0 %all-to-all-start.3 = ((f32[32,1,384]{2,1,0:T(1,128)}), f32[32,1,384]{2,1,0:T(1,128)S(1)}, u32[]{:S(2)}, u32[]{:S(2)}) async-start(f32[32,1,384]{2,1,0:T(1,128)} %reshape.413), calls=%async_computation.3 | async-start | bytes 98304 | tf_op jit(solution)/shard_map/all_to_all | solution.py:102
  128.3 8.8 %all-to-all-done.3 = f32[32,1,384]{2,1,0:T(1,128)S(1)} async-done(((f32[32,1,384]{2,1,0:T(1,128)}), f32[32,1,384]{2,1,0:T(1,128)S(1)}, u32[]{:S(2)}, u32[]{:S(2)}) %all-to-all-start.3) | async-done | bytes 49184 | tf_op jit(solution)/shard_map/all_to_all | solution.py:102
  139.9 6.0 %convolution_reduce_fusion = f32[64,8,128]{2,0,1:T(8,128)S(1)} fusion(f32[8,128]{1,0:T(8,128)S(1)} %copy-done.5, f32[8,128]{1,0:T(8,128)S(1)} %broadcast_add_fusion, f32[384]{0:T(512)S(1)} %copy-done.6, bf16[384,4,64]{0,2,1:T(8,128)(2,1)S(1)} %select_reduce_fusion.1), kind=kOutput, calls=%fused_computation.36 | convolution fusion | flops 204275712 | bytes 468480 | tf_op jit(solution)/shard_map/btk,brc->tkrc/dot_general | solution.py:154
  147.6 18.2 %all_to_all.35 = f32[8,8,8,3,128]{4,2,1,3,0:T(8,128)S(1)} all-to-all(f32[8,8,8,3,128]{4,2,1,3,0:T(8,128)S(1)} %pad_maximum_fusion), channel_id=1, replica_groups=mesh['img'=8,'vol'=32] {'img'}, dimensions={0} | all-to-all | bytes 1572864 | tf_op jit(solution)/shard_map/all_to_all | solution.py:95
  168.0 5.0 %all-to-all-start.5 = ((f32[32,8,8,3,128]{4,2,3,1,0:T(8,128)}), f32[32,8,8,3,128]{4,2,3,1,0:T(8,128)}, u32[]{:S(2)}, u32[]{:S(2)}) async-start(f32[32,8,8,3,128]{4,2,3,1,0:T(8,128)} %broadcast_in_dim.167), calls=%async_computation.5 | async-start | bytes 6291456 | tf_op jit(solution)/shard_map/all_to_all | solution.py:102
  173.8 70.0 %all-to-all-done.5 = f32[32,8,8,3,128]{4,2,3,1,0:T(8,128)} async-done(((f32[32,8,8,3,128]{4,2,3,1,0:T(8,128)}), f32[32,8,8,3,128]{4,2,3,1,0:T(8,128)}, u32[]{:S(2)}, u32[]{:S(2)}) %all-to-all-start.5) | async-done | bytes 3145760 | tf_op jit(solution)/shard_map/all_to_all | solution.py:102
  246.0 17.6 %scatter_custom_fusion = f32[2049,384]{1,0:T(8,128)} fusion(s32[2048]{0:T(1024)S(1)} %bitcast.172, f32[2048,384]{1,0:T(8,128)S(1)} %bitcast.151, f32[]{:T(128)} %constant.33.clone.1, f32[2048]{0:T(1024)S(1)} %bitcast.166), kind=kCustom, calls=%fused_computation.6 | custom fusion | flops 1572864 | bytes 6301188 | tf_op jit(solution)/shard_map/scatter-add | solution.py:87
  263.5 19.3 %scatter_custom_fusion.1 = f32[2049,384]{1,0:T(8,128)} fusion(f32[2049,384]{1,0:T(8,128)} %scatter_custom_fusion, s32[2048]{0:T(1024)S(1)} %bitcast.171, f32[2048,384]{1,0:T(8,128)S(1)} %bitcast.152, f32[2048]{0:T(1024)S(1)} %broadcast_subtract_fusion), kind=kCustom, calls=%fused_computation.4 | custom fusion | flops 1572864 | bytes 6301184 | tf_op jit(solution)/shard_map/scatter-add | solution.py:88
  284.9 3.0 reshape_reshape.7
  287.9 2.6 copy.122
  290.5 45.1 %all_to_all.36 = f32[8,8,32,3,128]{4,2,3,0,1:T(8,128)S(1)} all-to-all(f32[8,8,32,3,128]{4,2,3,0,1:T(8,128)S(1)} %copy.122), channel_id=1, replica_groups=mesh['img'=8,'vol'=32] {'img'}, dimensions={1} | all-to-all | bytes 6291456 | tf_op jit(solution)/shard_map/all_to_all | solution.py:95
  (92 shorter events, 30.6 us)
Async XLA Ops:
  38.1 15.2 %copy-start.5 = (f32[8,128]{1,0:T(8,128)S(1)}, f32[8,128]{1,0:T(8,128)}, u32[]{:S(2)}) copy-start(f32[8,128]{1,0:T(8,128)} %param.16) | copy-start | bytes 12292
  38.1 15.2 %copy-start.6 = (f32[384]{0:T(512)S(1)}, f32[384]{0:T(512)}, u32[]{:S(2)}) copy-start(f32[384]{0:T(512)} %param.13) | copy-start | bytes 4612
  40.7 37.1 %all-to-all-start = ((bf16[2,8,32,8,128]{4,0,3,1,2:T(2,128)(2,1)}), bf16[2,8,32,8,128]{4,0,3,1,2:T(2,128)(2,1)}, u32[]{:S(2)}, u32[]{:S(2)}) async-start(bf16[2,8,32,8,128]{4,0,3,1,2:T(2,128)(2,1)} %copy.105), calls=%async_computation | async-start | bytes 2097152 | tf_op jit(solution)/shard_map/all_to_all | solution.py:95
  53.3 6.7 %copy-start.4 = (s32[384]{0:T(512)S(1)}, s32[384]{0:T(512)}, u32[]{:S(2)}) copy-start(s32[384]{0:T(512)} %param.15) | copy-start | bytes 4612
  53.3 7.1 %copy-start = (bf16[2,384,8,128]{3,2,1,0:T(8,128)(2,1)S(1)}, bf16[2,384,8,128]{3,2,1,0:T(8,128)(2,1)}, u32[]{:S(2)}) copy-start(bf16[2,384,8,128]{3,2,1,0:T(8,128)(2,1)} %param.12) | copy-start | bytes 4718596
  61.9 28.6 %copy-start.3 = (s32[384,8]{0,1:T(8,128)S(1)}, s32[384,8]{0,1:T(8,128)}, u32[]{:S(2)}) copy-start(s32[384,8]{0,1:T(8,128)} %param.14) | copy-start | bytes 36868
  80.7 16.3 %all-to-all-start.1 = ((bf16[8,2,8,8,128]{4,2,3,1,0:T(8,128)(2,1)}), bf16[8,2,8,8,128]{4,2,3,1,0:T(8,128)(2,1)S(1)}, u32[]{:S(2)}, u32[]{:S(2)}) async-start(bf16[8,2,8,8,128]{4,2,3,1,0:T(8,128)(2,1)} %broadcast_in_dim.101), calls=%async_computation.1 | async-start | bytes 524288 | tf_op jit(solution)/shard_map/all_to_all | solution.py:102
  103.2 1.4 copy-start.2
  107.6 13.6 %all-to-all-start.2 = ((f32[32,1,384]{2,1,0:T(1,128)}), f32[32,1,384]{2,1,0:T(1,128)S(1)}, u32[]{:S(2)}, u32[]{:S(2)}) async-start(f32[32,1,384]{2,1,0:T(1,128)} %reshape.411), calls=%async_computation.2 | async-start | bytes 98304 | tf_op jit(solution)/shard_map/all_to_all | solution.py:95
  124.2 12.8 %all-to-all-start.3 = ((f32[32,1,384]{2,1,0:T(1,128)}), f32[32,1,384]{2,1,0:T(1,128)S(1)}, u32[]{:S(2)}, u32[]{:S(2)}) async-start(f32[32,1,384]{2,1,0:T(1,128)} %reshape.413), calls=%async_computation.3 | async-start | bytes 98304 | tf_op jit(solution)/shard_map/all_to_all | solution.py:102
  139.5 6.4 %copy-start.1 = (bf16[2,384,8,128,1]{3,2,1,0,4:T(8,128)(2,1)S(1)}, bf16[2,384,8,128,1]{3,2,1,0,4:T(8,128)(2,1)}, u32[]{:S(2)}) copy-start(bf16[2,384,8,128,1]{3,2,1,0,4:T(8,128)(2,1)} %fusion.59) | copy-start | bytes 4718596
  168.0 75.9 %all-to-all-start.5 = ((f32[32,8,8,3,128]{4,2,3,1,0:T(8,128)}), f32[32,8,8,3,128]{4,2,3,1,0:T(8,128)}, u32[]{:S(2)}, u32[]{:S(2)}) async-start(f32[32,8,8,3,128]{4,2,3,1,0:T(8,128)} %broadcast_in_dim.167), calls=%async_computation.5 | async-start | bytes 6291456 | tf_op jit(solution)/shard_map/all_to_all | solution.py:102

commit v3 on v2

--- a/solution.py
+++ b/solution.py
@@ -164,7 +164,7 @@
     initial = jnp.zeros((planes_here * ROWS + 1, 3 * COLS), jnp.float32)
     inserted = insert_into(
         initial,
-        gather_all(partial_value, "vol", 1),
+        gather_all(partial_value.astype(jnp.bfloat16), "vol", 1).astype(jnp.float32),
         plane_share,
         line_share,
         weight_share,

time: 343 us -> 306 us (0.89)
  waiting for transfers between devices: 108 us -> 74.2 us
    all_to_all x3, waiting for transfers between devices: 85.2 us -> 51 us  [gather_all(): lax.all_to_all(copies, axis_name, 0, 0, tiled=True)]
  transfers between devices with their start and end apart: 5 -> 5, of which waited for: 5 -> 5; matrix products, arithmetic and copies ran while one was open for 3% -> 4% of each run, Pallas kernels for 0% -> 0%
where the time goes in v3:
time: 306 us; the launch traced here: 301 us
  waiting for transfers between devices  74.2 us (24%)
  blocking collectives  62.2 us (20%)
  other arithmetic  61.9 us (20%)
  local copies, waits for them, and re-layouts  52.7 us (17%)
  starting transfers between devices  36 us (12%)
  matrix products  13.5 us (4%)
    all_to_all x2, blocking collectives, scatter_sum(): received = lax.all_to_all(split, axis_name, dim, dim, tiled=True)  62.2 us
    all_to_all x3, waiting for transfers between devices, gather_all(): lax.all_to_all(copies, axis_name, 0, 0, tiled=True)  51 us
    all_to_all x2, waiting for transfers between devices, scatter_sum(): received = lax.all_to_all(split, axis_name, dim, dim, tiled=True)  23.2 us
    scatter-add x1, other arithmetic, insert_into(): return carry.at[upper_index].add((1.0 - weight) * values)  19.2 us
    all_to_all x3, starting transfers between devices, gather_all(): lax.all_to_all(copies, axis_name, 0, 0, tiled=True)  18.8 us
    scatter-add x1, other arithmetic, insert_into(): carry = carry.at[lower_index].add(weight * values)  17.6 us
    all_to_all x2, starting transfers between devices, scatter_sum(): received = lax.all_to_all(split, axis_name, dim, dim, tiled=True)  17.2 us
    gather x1, local copies, waits for them, and re-layouts, extract_rows(): upper = jnp.take(flat, line_index + 1, axis=1)  14.4 us
  transfers between devices with their start and end apart: 5, of which 5 were waited for; matrix products, arithmetic and copies ran while one was open for 4% of the time, Pallas kernels for 0%

profile of v3, /device:TPU:1, one launch (start us, length us, event | category | flops | bytes accessed | tf_op | source)
XLA Modules:
  0.0 301.3 jit_solution(1587914001758756576)
XLA Ops:
  1.5 3.2 %copy.102 = f32[2,8,256,128]{3,0,2,1:T(2,128)S(1)} copy(f32[2,8,256,128]{3,2,1,0:T(8,128)} %param.17) | data formatting | bytes 4194304 | tf_op args[5]
  4.7 14.4 %gather_fusion = f32[2048,2,128]{2,1,0:T(2,128)} fusion(f32[2,2048,128]{2,0,1:T(2,128)S(1)} %bitcast.153, s32[2048]{0:T(1024)S(1)} %broadcast_clamp_fusion.1), kind=kCustom, calls=%fused_computation.clone | custom fusion | bytes 4202496 | tf_op jit(solution)/shard_map/jit(_take)/gather | solution.py:62
  19.2 14.4 %gather_fusion.1 = f32[2048,2,128]{2,1,0:T(2,128)} fusion(f32[2,2048,128]{2,0,1:T(2,128)S(1)} %bitcast.154, s32[2048]{0:T(1024)S(1)} %broadcast_clamp_fusion), kind=kCustom, calls=%fused_computation.1.clone | custom fusion | bytes 4202496 | tf_op jit(solution)/shard_map/jit(_take)/gather | solution.py:63
  34.3 3.8 %fusion.6 = bf16[2,8,256,128]{3,2,1,0:T(8,128)(2,1)S(1)} fusion(f32[8,256,2,128]{3,2,1,0:T(2,128)} %bitcast.156, f32[8,256,2,128]{3,2,1,0:T(2,128)} %bitcast.155, f32[8,256]{1,0:T(8,128)S(1)} %get-tuple-element.12, f32[8,256]{1,0:T(8,128)S(1)} %get-tuple-element.13, pred[8,256]{1,0:T(8,128)(4,1)S(1)} %compare_and_fusion, ...), kind=kLoop, calls=%fused_computation.15 | loop fusion | flops 3670016 | bytes 5265408 | tf_op jit(solution)/shard_map/convert_element_type | solution.py:66
  38.1 2.6 copy.105
  40.7 12.5 %all-to-all-start = ((bf16[2,8,32,8,128]{4,0,3,1,2:T(2,128)(2,1)}), bf16[2,8,32,8,128]{4,0,3,1,2:T(2,128)(2,1)}, u32[]{:S(2)}, u32[]{:S(2)}) async-start(bf16[2,8,32,8,128]{4,0,3,1,2:T(2,128)(2,1)} %copy.105), calls=%async_computation | async-start | bytes 2097152 | tf_op jit(solution)/shard_map/all_to_all | solution.py:95
  53.3 5.7 %fusion.13 = f32[384,8,128]{2,0,1:T(8,128)S(1)} fusion(f32[8,128]{1,0:T(8,128)S(1)} %copy-done.5, f32[8,128]{1,0:T(8,128)S(1)} %broadcast_add_fusion, f32[384]{0:T(512)S(1)} %copy-done.6), kind=kLoop, calls=%fused_computation.26 | loop fusion | flops 2359296 | bytes 1582592 | tf_op jit(solution)/shard_map/mul | solution.py:136
  63.3 14.5 %all-to-all-done = bf16[2,8,32,8,128]{4,0,3,1,2:T(2,128)(2,1)} async-done(((bf16[2,8,32,8,128]{4,0,3,1,2:T(2,128)(2,1)}), bf16[2,8,32,8,128]{4,0,3,1,2:T(2,128)(2,1)}, u32[]{:S(2)}, u32[]{:S(2)}) %all-to-all-start) | async-done | bytes 1048608 | tf_op jit(solution)/shard_map/all_to_all | solution.py:95
  80.7 9.8 %all-to-all-start.1 = ((bf16[8,2,8,8,128]{4,2,3,1,0:T(8,128)(2,1)}), bf16[8,2,8,8,128]{4,2,3,1,0:T(8,128)(2,1)S(1)}, u32[]{:S(2)}, u32[]{:S(2)}) async-start(bf16[8,2,8,8,128]{4,2,3,1,0:T(8,128)(2,1)} %broadcast_in_dim.101), calls=%async_computation.1 | async-start | bytes 524288 | tf_op jit(solution)/shard_map/all_to_all | solution.py:102
  90.6 6.3 %all-to-all-done.1 = bf16[8,2,8,8,128]{4,2,3,1,0:T(8,128)(2,1)S(1)} async-done(((bf16[8,2,8,8,128]{4,2,3,1,0:T(8,128)(2,1)}), bf16[8,2,8,8,128]{4,2,3,1,0:T(8,128)(2,1)S(1)}, u32[]{:S(2)}, u32[]{:S(2)}) %all-to-all-start.1) | async-done | bytes 262176 | tf_op jit(solution)/shard_map/all_to_all | solution.py:102
  97.2 6.0 %fusion.28 = f32[384,64]{0,1:T(8,128)S(1)} fusion(f32[8,128]{1,0:T(8,128)S(1)} %copy-done.5, f32[8,128]{1,0:T(8,128)S(1)} %broadcast_add_fusion, f32[384]{0:T(512)S(1)} %copy-done.6, bf16[64,8,128]{2,1,0:T(8,128)(2,1)S(1)} %add_convert_fusion.1), kind=kOutput, calls=%fused_computation.41 | convolution fusion | flops 53108736 | bytes 239104 | tf_op jit(solution)/shard_map/brc,krc->bk/dot_general | solution.py:139
  107.6 4.8 %all-to-all-start.2 = ((f32[32,1,384]{2,1,0:T(1,128)}), f32[32,1,384]{2,1,0:T(1,128)S(1)}, u32[]{:S(2)}, u32[]{:S(2)}) async-start(f32[32,1,384]{2,1,0:T(1,128)} %reshape.419), calls=%async_computation.2 | async-start | bytes 98304 | tf_op jit(solution)/shard_map/all_to_all | solution.py:95
  112.4 8.8 %all-to-all-done.2 = f32[32,1,384]{2,1,0:T(1,128)S(1)} async-done(((f32[32,1,384]{2,1,0:T(1,128)}), f32[32,1,384]{2,1,0:T(1,128)S(1)}, u32[]{:S(2)}, u32[]{:S(2)}) %all-to-all-start.2) | async-done | bytes 49184 | tf_op jit(solution)/shard_map/all_to_all | solution.py:95
  124.2 4.0 %all-to-all-start.3 = ((f32[32,1,384]{2,1,0:T(1,128)}), f32[32,1,384]{2,1,0:T(1,128)S(1)}, u32[]{:S(2)}, u32[]{:S(2)}) async-start(f32[32,1,384]{2,1,0:T(1,128)} %reshape.421), calls=%async_computation.3 | async-start | bytes 98304 | tf_op jit(solution)/shard_map/all_to_all | solution.py:102
  128.3 8.8 %all-to-all-done.3 = f32[32,1,384]{2,1,0:T(1,128)S(1)} async-done(((f32[32,1,384]{2,1,0:T(1,128)}), f32[32,1,384]{2,1,0:T(1,128)S(1)}, u32[]{:S(2)}, u32[]{:S(2)}) %all-to-all-start.3) | async-done | bytes 49184 | tf_op jit(solution)/shard_map/all_to_all | solution.py:102
  139.9 6.0 %convolution_reduce_fusion = f32[64,8,128]{2,0,1:T(8,128)S(1)} fusion(f32[8,128]{1,0:T(8,128)S(1)} %copy-done.5, f32[8,128]{1,0:T(8,128)S(1)} %broadcast_add_fusion, f32[384]{0:T(512)S(1)} %copy-done.6, bf16[384,4,64]{0,2,1:T(8,128)(2,1)S(1)} %select_reduce_fusion.1), kind=kOutput, calls=%fused_computation.37 | convolution fusion | flops 204275712 | bytes 468480 | tf_op jit(solution)/shard_map/btk,brc->tkrc/dot_general | solution.py:154
  147.6 18.2 %all_to_all.35 = f32[8,8,8,3,128]{4,2,1,3,0:T(8,128)S(1)} all-to-all(f32[8,8,8,3,128]{4,2,1,3,0:T(8,128)S(1)} %pad_maximum_fusion), channel_id=1, replica_groups=mesh['img'=8,'vol'=32] {'img'}, dimensions={0} | all-to-all | bytes 1572864 | tf_op jit(solution)/shard_map/all_to_all | solution.py:95
  167.4 4.9 %all-to-all-start.5 = ((bf16[32,8,8,3,128]{4,2,3,1,0:T(8,128)(2,1)}), bf16[32,8,8,3,128]{4,2,3,1,0:T(8,128)(2,1)}, u32[]{:S(2)}, u32[]{:S(2)}) async-start(bf16[32,8,8,3,128]{4,2,3,1,0:T(8,128)(2,1)} %broadcast_in_dim.167), calls=%async_computation.5 | async-start | bytes 3145728 | tf_op jit(solution)/shard_map/all_to_all | solution.py:102
  173.2 35.9 %all-to-all-done.5 = bf16[32,8,8,3,128]{4,2,3,1,0:T(8,128)(2,1)} async-done(((bf16[32,8,8,3,128]{4,2,3,1,0:T(8,128)(2,1)}), bf16[32,8,8,3,128]{4,2,3,1,0:T(8,128)(2,1)}, u32[]{:S(2)}, u32[]{:S(2)}) %all-to-all-start.5) | async-done | bytes 1572896 | tf_op jit(solution)/shard_map/all_to_all | solution.py:102
  210.6 17.6 %scatter_custom_fusion = f32[2049,384]{1,0:T(8,128)} fusion(s32[2048]{0:T(1024)S(1)} %bitcast.172, f32[2048,384]{1,0:T(8,128)S(1)} %bitcast.151, f32[]{:T(128)} %constant.33.clone.1, f32[2048]{0:T(1024)S(1)} %bitcast.166), kind=kCustom, calls=%fused_computation.6 | custom fusion | flops 1572864 | bytes 6301188 | tf_op jit(solution)/shard_map/scatter-add | solution.py:87
  228.2 19.2 %scatter_custom_fusion.1 = f32[2049,384]{1,0:T(8,128)} fusion(f32[2049,384]{1,0:T(8,128)} %scatter_custom_fusion, s32[2048]{0:T(1024)S(1)} %bitcast.171, f32[2048,384]{1,0:T(8,128)S(1)} %bitcast.152, f32[2048]{0:T(1024)S(1)} %broadcast_subtract_fusion), kind=kCustom, calls=%fused_computation.4 | custom fusion | flops 1572864 | bytes 6301184 | tf_op jit(solution)/shard_map/scatter-add | solution.py:88
  249.5 3.0 reshape_reshape.3
  252.5 2.6 copy.122
  255.1 44.0 %all_to_all.36 = f32[8,8,32,3,128]{4,2,3,0,1:T(8,128)S(1)} all-to-all(f32[8,8,32,3,128]{4,2,3,0,1:T(8,128)S(1)} %copy.122), channel_id=1, replica_groups=mesh['img'=8,'vol'=32] {'img'}, dimensions={1} | all-to-all | bytes 6291456 | tf_op jit(solution)/shard_map/all_to_all | solution.py:95
  (92 shorter events, 29.5 us)
Async XLA Ops:
  38.1 15.2 %copy-start.5 = (f32[8,128]{1,0:T(8,128)S(1)}, f32[8,128]{1,0:T(8,128)}, u32[]{:S(2)}) copy-start(f32[8,128]{1,0:T(8,128)} %param.16) | copy-start | bytes 12292
  38.1 15.2 %copy-start.6 = (f32[384]{0:T(512)S(1)}, f32[384]{0:T(512)}, u32[]{:S(2)}) copy-start(f32[384]{0:T(512)} %param.13) | copy-start | bytes 4612
  40.7 37.1 %all-to-all-start = ((bf16[2,8,32,8,128]{4,0,3,1,2:T(2,128)(2,1)}), bf16[2,8,32,8,128]{4,0,3,1,2:T(2,128)(2,1)}, u32[]{:S(2)}, u32[]{:S(2)}) async-start(bf16[2,8,32,8,128]{4,0,3,1,2:T(2,128)(2,1)} %copy.105), calls=%async_computation | async-start | bytes 2097152 | tf_op jit(solution)/shard_map/all_to_all | solution.py:95
  53.3 6.7 %copy-start.4 = (s32[384]{0:T(512)S(1)}, s32[384]{0:T(512)}, u32[]{:S(2)}) copy-start(s32[384]{0:T(512)} %param.15) | copy-start | bytes 4612
  53.3 7.1 %copy-start = (bf16[2,384,8,128]{3,2,1,0:T(8,128)(2,1)S(1)}, bf16[2,384,8,128]{3,2,1,0:T(8,128)(2,1)}, u32[]{:S(2)}) copy-start(bf16[2,384,8,128]{3,2,1,0:T(8,128)(2,1)} %param.12) | copy-start | bytes 4718596
  61.9 28.6 %copy-start.3 = (s32[384,8]{0,1:T(8,128)S(1)}, s32[384,8]{0,1:T(8,128)}, u32[]{:S(2)}) copy-start(s32[384,8]{0,1:T(8,128)} %param.14) | copy-start | bytes 36868
  80.7 16.3 %all-to-all-start.1 = ((bf16[8,2,8,8,128]{4,2,3,1,0:T(8,128)(2,1)}), bf16[8,2,8,8,128]{4,2,3,1,0:T(8,128)(2,1)S(1)}, u32[]{:S(2)}, u32[]{:S(2)}) async-start(bf16[8,2,8,8,128]{4,2,3,1,0:T(8,128)(2,1)} %broadcast_in_dim.101), calls=%async_computation.1 | async-start | bytes 524288 | tf_op jit(solution)/shard_map/all_to_all | solution.py:102
  103.2 1.4 copy-start.2
  107.6 13.6 %all-to-all-start.2 = ((f32[32,1,384]{2,1,0:T(1,128)}), f32[32,1,384]{2,1,0:T(1,128)S(1)}, u32[]{:S(2)}, u32[]{:S(2)}) async-start(f32[32,1,384]{2,1,0:T(1,128)} %reshape.419), calls=%async_computation.2 | async-start | bytes 98304 | tf_op jit(solution)/shard_map/all_to_all | solution.py:95
  124.2 12.8 %all-to-all-start.3 = ((f32[32,1,384]{2,1,0:T(1,128)}), f32[32,1,384]{2,1,0:T(1,128)S(1)}, u32[]{:S(2)}, u32[]{:S(2)}) async-start(f32[32,1,384]{2,1,0:T(1,128)} %reshape.421), calls=%async_computation.3 | async-start | bytes 98304 | tf_op jit(solution)/shard_map/all_to_all | solution.py:102
  139.5 6.4 %copy-start.1 = (bf16[2,384,8,128,1]{3,2,1,0,4:T(8,128)(2,1)S(1)}, bf16[2,384,8,128,1]{3,2,1,0,4:T(8,128)(2,1)}, u32[]{:S(2)}) copy-start(bf16[2,384,8,128,1]{3,2,1,0,4:T(8,128)(2,1)} %fusion.59) | copy-start | bytes 4718596
  167.4 41.6 %all-to-all-start.5 = ((bf16[32,8,8,3,128]{4,2,3,1,0:T(8,128)(2,1)}), bf16[32,8,8,3,128]{4,2,3,1,0:T(8,128)(2,1)}, u32[]{:S(2)}, u32[]{:S(2)}) async-start(bf16[32,8,8,3,128]{4,2,3,1,0:T(8,128)(2,1)} %broadcast_in_dim.167), calls=%async_computation.5 | async-start | bytes 3145728 | tf_op jit(solution)/shard_map/all_to_all | solution.py:102

commit v4 on v3

--- a/solution.py
+++ b/solution.py
@@ -3,6 +3,8 @@
 import jax
 import jax.numpy as jnp
 from jax import lax
+from jax.experimental import pallas as pl
+from jax.experimental.pallas import tpu as pltpu
 from jax.sharding import PartitionSpec as P
 
 ROWS = 256
@@ -101,6 +103,47 @@
     copies = jnp.broadcast_to(x[None], (count,) + x.shape)
     received = jnp.moveaxis(lax.all_to_all(copies, axis_name, 0, 0, tiled=True), 0, dim)
     return received.reshape(x.shape[:dim] + (count * x.shape[dim],) + x.shape[dim + 1 :])
+
+
+def insert_kernel(start_ref, weight_ref, value_ref, out_ref):
+    lines = out_ref.shape[0]
+    rows = value_ref.shape[0]
+    chunk = 512
+    first_slot = pl.program_id(0) * lines
+    slot = first_slot + lax.broadcasted_iota(jnp.int32, (lines, chunk), 0)
+    total = jnp.zeros(out_ref.shape, jnp.float32)
+    for part in range(rows // chunk):
+        cols = pl.ds(part * chunk, chunk)
+        start = start_ref[:, cols]
+        weight = weight_ref[:, cols]
+        spread = jnp.where(slot == start, weight, jnp.where(slot == start + 1, 1.0 - weight, 0.0))
+        high = spread.astype(jnp.bfloat16)
+        low = (spread - high.astype(jnp.float32)).astype(jnp.bfloat16)
+        block = value_ref[cols, :]
+        total += jnp.dot(high, block, preferred_element_type=jnp.float32)
+        total += jnp.dot(low, block, preferred_element_type=jnp.float32)
+    out_ref[...] = total
+
+
+def insert_rows(values, start, weight, planes_here):
+    rows, width = values.shape
+    return pl.pallas_call(
+        insert_kernel,
+        grid=(planes_here,),
+        in_specs=[
+            pl.BlockSpec((1, rows), lambda q: (0, 0)),
+            pl.BlockSpec((1, rows), lambda q: (0, 0)),
+            pl.BlockSpec((rows, width), lambda q: (0, 0)),
+        ],
+        out_specs=pl.BlockSpec((ROWS, width), lambda q: (q, 0)),
+        out_shape=jax.ShapeDtypeStruct((planes_here * ROWS, width), jnp.float32),
+        compiler_params=pltpu.CompilerParams(vmem_limit_bytes=48 * 1024 * 1024),
+        cost_estimate=pl.CostEstimate(
+            flops=4 * planes_here * ROWS * rows * width,
+            bytes_accessed=rows * width * 2 + planes_here * ROWS * width * 4,
+            transcendentals=0,
+        ),
+    )(start.reshape(1, rows), weight.reshape(1, rows), values)
 
 
 def body(
@@ -161,19 +204,14 @@
     partial_value = scatter_sum(
         jnp.stack([num_re, num_im, jnp.sum(d_part, axis=0)], axis=2), "img", 0
     )
-    initial = jnp.zeros((planes_here * ROWS + 1, 3 * COLS), jnp.float32)
-    inserted = insert_into(
-        initial,
-        gather_all(partial_value.astype(jnp.bfloat16), "vol", 1).astype(jnp.float32),
-        plane_share,
-        line_share,
-        weight_share,
-        slab_id,
-        planes_here,
-        0,
-        ROWS,
-    )
-    slab = inserted[: planes_here * ROWS].reshape(planes_here, ROWS, 3, COLS)
+    local_plane = plane_share - slab_id * planes_here
+    in_slab = (local_plane >= 0) & (local_plane < planes_here)
+    start = jnp.where(in_slab, local_plane * ROWS + line_share, -2)
+    piece = gather_all(partial_value.astype(jnp.bfloat16), "vol", 1)
+    inserted = insert_rows(
+        piece.reshape(share * ROWS, 3 * COLS), start.reshape(-1), weight_share.reshape(-1), planes_here
+    )
+    slab = inserted.reshape(planes_here, ROWS, 3, COLS)
     summed = scatter_sum(slab, "img", 1)
     denom = summed[:, :, 2] + regularizer
     return jnp.stack([summed[:, :, 0] / denom, summed[:, :, 1] / denom], axis=0)

time: 306 us -> 275 us (0.90)
  other arithmetic: 61.9 us -> 22.7 us
  Pallas kernels: 0 us -> 9.99 us
    scatter-add x2 -> x0, other arithmetic: 36.8 us -> none  [the longest x1 19.2 us: insert_into(): return carry.at[upper_index].add((1.0 - weight) * values)]
    pallas_call x0 -> x1, Pallas kernels: none -> 9.99 us  [insert_rows(): pl.pallas_call(insert_kernel, grid=(planes_here,), in_specs=[pl.BlockSpec...]
    unnamed x25 -> x24, local copies, waits for them, and re-layouts: 7.51 us -> 7.57 us
where the time goes in v4:
time: 275 us; the launch traced here: 270 us
  waiting for transfers between devices  75 us (27%)
  blocking collectives  62.2 us (23%)
  local copies, waits for them, and re-layouts  51 us (19%)
  starting transfers between devices  35.4 us (13%)
  other arithmetic  22.7 us (8%)
  matrix products  13.5 us (5%)
  Pallas kernels  9.99 us (4%)
    all_to_all x2, blocking collectives, scatter_sum(): received = lax.all_to_all(split, axis_name, dim, dim, tiled=True)  62.2 us
    all_to_all x3, waiting for transfers between devices, gather_all(): lax.all_to_all(copies, axis_name, 0, 0, tiled=True)  51.8 us
    all_to_all x2, waiting for transfers between devices, scatter_sum(): received = lax.all_to_all(split, axis_name, dim, dim, tiled=True)  23.2 us
    all_to_all x3, starting transfers between devices, gather_all(): lax.all_to_all(copies, axis_name, 0, 0, tiled=True)  18 us
    all_to_all x2, starting transfers between devices, scatter_sum(): received = lax.all_to_all(split, axis_name, dim, dim, tiled=True)  17.4 us
    gather x1, local copies, waits for them, and re-layouts, extract_rows(): upper = jnp.take(flat, line_index + 1, axis=1)  14.4 us
    gather x1, local copies, waits for them, and re-layouts, extract_rows(): lower = jnp.take(flat, line_index, axis=1)  14.4 us
    pallas_call x1, Pallas kernels, insert_rows(): pl.pallas_call(insert_kernel, grid=(planes_here,), in_specs=[pl.BlockSpec...  9.99 us
  transfers between devices with their start and end apart: 5, of which 5 were waited for; matrix products, arithmetic and copies ran while one was open for 4% of the time, Pallas kernels for 0%

profile of v4, /device:TPU:1, one launch (start us, length us, event | category | flops | bytes accessed | tf_op | source)
XLA Modules:
  0.0 270.5 jit_solution(11893550510930342551)
XLA Ops:
  1.5 3.2 %copy.103 = f32[2,8,256,128]{3,0,2,1:T(2,128)S(1)} copy(f32[2,8,256,128]{3,2,1,0:T(8,128)} %param.17) | data formatting | bytes 4194304 | tf_op args[5]
  4.7 14.4 %gather_fusion = f32[2048,2,128]{2,1,0:T(2,128)} fusion(f32[2,2048,128]{2,0,1:T(2,128)S(1)} %bitcast.146, s32[2048]{0:T(1024)S(1)} %broadcast_clamp_fusion.1), kind=kCustom, calls=%fused_computation.clone | custom fusion | bytes 4202496 | tf_op jit(solution)/shard_map/jit(_take)/gather | solution.py:64
  19.2 14.4 %gather_fusion.1 = f32[2048,2,128]{2,1,0:T(2,128)} fusion(f32[2,2048,128]{2,0,1:T(2,128)S(1)} %bitcast.147, s32[2048]{0:T(1024)S(1)} %broadcast_clamp_fusion), kind=kCustom, calls=%fused_computation.1.clone | custom fusion | bytes 4202496 | tf_op jit(solution)/shard_map/jit(_take)/gather | solution.py:65
  34.3 3.8 %fusion.2 = bf16[2,8,256,128]{3,2,1,0:T(8,128)(2,1)S(1)} fusion(f32[8,256,2,128]{3,2,1,0:T(2,128)} %bitcast.149, f32[8,256,2,128]{3,2,1,0:T(2,128)} %bitcast.148, f32[8,256]{1,0:T(8,128)S(1)} %get-tuple-element.10, f32[8,256]{1,0:T(8,128)S(1)} %get-tuple-element.11, pred[8,256]{1,0:T(8,128)(4,1)S(1)} %compare_and_fusion, ...), kind=kLoop, calls=%fused_computation.9 | loop fusion | flops 3670016 | bytes 5265408 | tf_op jit(solution)/shard_map/convert_element_type | solution.py:68
  38.1 2.6 copy.106
  40.7 12.6 %all-to-all-start = ((bf16[2,8,32,8,128]{4,0,3,1,2:T(2,128)(2,1)}), bf16[2,8,32,8,128]{4,0,3,1,2:T(2,128)(2,1)}, u32[]{:S(2)}, u32[]{:S(2)}) async-start(bf16[2,8,32,8,128]{4,0,3,1,2:T(2,128)(2,1)} %copy.106), calls=%async_computation | async-start | bytes 2097152 | tf_op jit(solution)/shard_map/all_to_all | solution.py:97
  53.4 5.7 %fusion.8 = f32[384,8,128]{2,0,1:T(8,128)S(1)} fusion(f32[8,128]{1,0:T(8,128)S(1)} %copy-done.5, f32[8,128]{1,0:T(8,128)S(1)} %broadcast_add_fusion, f32[384]{0:T(512)S(1)} %copy-done.6), kind=kLoop, calls=%fused_computation.19 | loop fusion | flops 2359296 | bytes 1582592 | tf_op jit(solution)/shard_map/mul | solution.py:179
  63.5 14.4 %all-to-all-done = bf16[2,8,32,8,128]{4,0,3,1,2:T(2,128)(2,1)} async-done(((bf16[2,8,32,8,128]{4,0,3,1,2:T(2,128)(2,1)}), bf16[2,8,32,8,128]{4,0,3,1,2:T(2,128)(2,1)}, u32[]{:S(2)}, u32[]{:S(2)}) %all-to-all-start) | async-done | bytes 1048608 | tf_op jit(solution)/shard_map/all_to_all | solution.py:97
  77.9 2.1 reduce_sum.96
  80.8 9.8 %all-to-all-start.1 = ((bf16[8,2,8,8,128]{4,2,3,1,0:T(8,128)(2,1)}), bf16[8,2,8,8,128]{4,2,3,1,0:T(8,128)(2,1)S(1)}, u32[]{:S(2)}, u32[]{:S(2)}) async-start(bf16[8,2,8,8,128]{4,2,3,1,0:T(8,128)(2,1)} %broadcast_in_dim.97), calls=%async_computation.1 | async-start | bytes 524288 | tf_op jit(solution)/shard_map/all_to_all | solution.py:104
  90.7 6.3 %all-to-all-done.1 = bf16[8,2,8,8,128]{4,2,3,1,0:T(8,128)(2,1)S(1)} async-done(((bf16[8,2,8,8,128]{4,2,3,1,0:T(8,128)(2,1)}), bf16[8,2,8,8,128]{4,2,3,1,0:T(8,128)(2,1)S(1)}, u32[]{:S(2)}, u32[]{:S(2)}) %all-to-all-start.1) | async-done | bytes 262176 | tf_op jit(solution)/shard_map/all_to_all | solution.py:104
  97.3 6.0 %fusion.21 = f32[384,64]{0,1:T(8,128)S(1)} fusion(f32[8,128]{1,0:T(8,128)S(1)} %copy-done.5, f32[8,128]{1,0:T(8,128)S(1)} %broadcast_add_fusion, f32[384]{0:T(512)S(1)} %copy-done.6, bf16[64,8,128]{2,1,0:T(8,128)(2,1)S(1)} %add_convert_fusion.1), kind=kOutput, calls=%fused_computation.31 | convolution fusion | flops 53108736 | bytes 239104 | tf_op jit(solution)/shard_map/brc,krc->bk/dot_general | solution.py:182
  107.7 4.8 %all-to-all-start.2 = ((f32[32,1,384]{2,1,0:T(1,128)}), f32[32,1,384]{2,1,0:T(1,128)S(1)}, u32[]{:S(2)}, u32[]{:S(2)}) async-start(f32[32,1,384]{2,1,0:T(1,128)} %reshape.320), calls=%async_computation.2 | async-start | bytes 98304 | tf_op jit(solution)/shard_map/all_to_all | solution.py:97
  112.5 8.8 %all-to-all-done.2 = f32[32,1,384]{2,1,0:T(1,128)S(1)} async-done(((f32[32,1,384]{2,1,0:T(1,128)}), f32[32,1,384]{2,1,0:T(1,128)S(1)}, u32[]{:S(2)}, u32[]{:S(2)}) %all-to-all-start.2) | async-done | bytes 49184 | tf_op jit(solution)/shard_map/all_to_all | solution.py:97
  124.3 4.0 %all-to-all-start.3 = ((f32[32,1,384]{2,1,0:T(1,128)}), f32[32,1,384]{2,1,0:T(1,128)S(1)}, u32[]{:S(2)}, u32[]{:S(2)}) async-start(f32[32,1,384]{2,1,0:T(1,128)} %reshape.322), calls=%async_computation.3 | async-start | bytes 98304 | tf_op jit(solution)/shard_map/all_to_all | solution.py:104
  128.4 8.8 %all-to-all-done.3 = f32[32,1,384]{2,1,0:T(1,128)S(1)} async-done(((f32[32,1,384]{2,1,0:T(1,128)}), f32[32,1,384]{2,1,0:T(1,128)S(1)}, u32[]{:S(2)}, u32[]{:S(2)}) %all-to-all-start.3) | async-done | bytes 49184 | tf_op jit(solution)/shard_map/all_to_all | solution.py:104
  140.0 6.0 %convolution_reduce_fusion = f32[64,8,128]{2,0,1:T(8,128)S(1)} fusion(f32[8,128]{1,0:T(8,128)S(1)} %copy-done.5, f32[8,128]{1,0:T(8,128)S(1)} %broadcast_add_fusion, f32[384]{0:T(512)S(1)} %copy-done.6, bf16[384,4,64]{0,2,1:T(8,128)(2,1)S(1)} %select_reduce_fusion.1), kind=kOutput, calls=%fused_computation.27 | convolution fusion | flops 204275712 | bytes 468480 | tf_op jit(solution)/shard_map/btk,brc->tkrc/dot_general | solution.py:197
  147.7 18.2 %all_to_all.35 = f32[8,8,8,3,128]{4,2,1,3,0:T(8,128)S(1)} all-to-all(f32[8,8,8,3,128]{4,2,1,3,0:T(8,128)S(1)} %pad_maximum_fusion), channel_id=1, replica_groups=mesh['img'=8,'vol'=32] {'img'}, dimensions={0} | all-to-all | bytes 1572864 | tf_op jit(solution)/shard_map/all_to_all | solution.py:97
  167.5 4.2 %all-to-all-start.5 = ((bf16[32,8,8,3,128]{4,2,3,1,0:T(8,128)(2,1)}), bf16[32,8,8,3,128]{4,2,3,1,0:T(8,128)(2,1)S(1)}, u32[]{:S(2)}, u32[]{:S(2)}) async-start(bf16[32,8,8,3,128]{4,2,3,1,0:T(8,128)(2,1)} %broadcast_in_dim.160), calls=%async_computation.5 | async-start | bytes 3145728 | tf_op jit(solution)/shard_map/all_to_all | solution.py:104
  171.7 36.7 %all-to-all-done.5 = bf16[32,8,8,3,128]{4,2,3,1,0:T(8,128)(2,1)S(1)} async-done(((bf16[32,8,8,3,128]{4,2,3,1,0:T(8,128)(2,1)}), bf16[32,8,8,3,128]{4,2,3,1,0:T(8,128)(2,1)S(1)}, u32[]{:S(2)}, u32[]{:S(2)}) %all-to-all-start.5) | async-done | bytes 1572896 | tf_op jit(solution)/shard_map/all_to_all | solution.py:104
  208.7 10.0 %shard_map.100 = f32[2048,384]{1,0:T(8,128)S(1)} custom-call(s32[1,2048]{1,0:T(1,128)S(1)} %bitcast.144, f32[1,2048]{1,0:T(1,128)S(1)} %bitcast.145, bf16[2048,384]{1,0:T(8,128)(2,1)S(1)} %bitcast.143), custom_call_target="tpu_custom_call" | custom-call | flops 6442450944 | bytes 4718592 | tf_op jit(solution)/shard_map/pallas_call | solution.py:130
  218.7 3.0 %reshape_reshape.15 = f32[8,8,32,3,128]{4,3,2,1,0:T(4,128)} reshape(f32[2048,384]{1,0:T(8,128)S(1)} %shard_map.100) | data formatting | bytes 6291456 | tf_op jit(solution)/shard_map/reshape;reshape | solution.py:96
  221.7 2.6 copy.123
  224.3 44.0 %all_to_all.36 = f32[8,8,32,3,128]{4,2,3,0,1:T(8,128)S(1)} all-to-all(f32[8,8,32,3,128]{4,2,3,0,1:T(8,128)S(1)} %copy.123), channel_id=1, replica_groups=mesh['img'=8,'vol'=32] {'img'}, dimensions={1} | all-to-all | bytes 6291456 | tf_op jit(solution)/shard_map/all_to_all | solution.py:97
  (85 shorter events, 23.3 us)
Async XLA Ops:
  40.7 12.7 %copy-start.5 = (f32[8,128]{1,0:T(8,128)S(1)}, f32[8,128]{1,0:T(8,128)}, u32[]{:S(2)}) copy-start(f32[8,128]{1,0:T(8,128)} %param.16) | copy-start | bytes 12292
  40.7 12.7 %copy-start.6 = (f32[384]{0:T(512)S(1)}, f32[384]{0:T(512)}, u32[]{:S(2)}) copy-start(f32[384]{0:T(512)} %param.13) | copy-start | bytes 4612
  40.7 37.2 %all-to-all-start = ((bf16[2,8,32,8,128]{4,0,3,1,2:T(2,128)(2,1)}), bf16[2,8,32,8,128]{4,0,3,1,2:T(2,128)(2,1)}, u32[]{:S(2)}, u32[]{:S(2)}) async-start(bf16[2,8,32,8,128]{4,0,3,1,2:T(2,128)(2,1)} %copy.106), calls=%async_computation | async-start | bytes 2097152 | tf_op jit(solution)/shard_map/all_to_all | solution.py:97
  59.1 0.9 copy-start.4
  59.2 1.4 copy-start
  63.5 27.1 %copy-start.3 = (s32[384,8]{0,1:T(8,128)S(1)}, s32[384,8]{0,1:T(8,128)}, u32[]{:S(2)}) copy-start(s32[384,8]{0,1:T(8,128)} %param.14) | copy-start | bytes 36868
  80.8 16.3 %all-to-all-start.1 = ((bf16[8,2,8,8,128]{4,2,3,1,0:T(8,128)(2,1)}), bf16[8,2,8,8,128]{4,2,3,1,0:T(8,128)(2,1)S(1)}, u32[]{:S(2)}, u32[]{:S(2)}) async-start(bf16[8,2,8,8,128]{4,2,3,1,0:T(8,128)(2,1)} %broadcast_in_dim.97), calls=%async_computation.1 | async-start | bytes 524288 | tf_op jit(solution)/shard_map/all_to_all | solution.py:104
  103.3 1.4 copy-start.2
  107.7 13.6 %all-to-all-start.2 = ((f32[32,1,384]{2,1,0:T(1,128)}), f32[32,1,384]{2,1,0:T(1,128)S(1)}, u32[]{:S(2)}, u32[]{:S(2)}) async-start(f32[32,1,384]{2,1,0:T(1,128)} %reshape.320), calls=%async_computation.2 | async-start | bytes 98304 | tf_op jit(solution)/shard_map/all_to_all | solution.py:97
  124.3 12.9 %all-to-all-start.3 = ((f32[32,1,384]{2,1,0:T(1,128)}), f32[32,1,384]{2,1,0:T(1,128)S(1)}, u32[]{:S(2)}, u32[]{:S(2)}) async-start(f32[32,1,384]{2,1,0:T(1,128)} %reshape.322), calls=%async_computation.3 | async-start | bytes 98304 | tf_op jit(solution)/shard_map/all_to_all | solution.py:104
  140.0 6.0 %copy-start.1 = (bf16[2,384,8,128,1]{3,2,1,0,4:T(8,128)(2,1)S(1)}, bf16[2,384,8,128,1]{3,2,1,0,4:T(8,128)(2,1)}, u32[]{:S(2)}) copy-start(bf16[2,384,8,128,1]{3,2,1,0,4:T(8,128)(2,1)} %fusion.52) | copy-start | bytes 4718596
  167.5 40.9 %all-to-all-start.5 = ((bf16[32,8,8,3,128]{4,2,3,1,0:T(8,128)(2,1)}), bf16[32,8,8,3,128]{4,2,3,1,0:T(8,128)(2,1)S(1)}, u32[]{:S(2)}, u32[]{:S(2)}) async-start(bf16[32,8,8,3,128]{4,2,3,1,0:T(8,128)(2,1)} %broadcast_in_dim.160), calls=%async_computation.5 | async-start | bytes 3145728 | tf_op jit(solution)/shard_map/all_to_all | solution.py:104

commit v5 on v4

--- a/solution.py
+++ b/solution.py
@@ -144,6 +144,55 @@
             transcendentals=0,
         ),
     )(start.reshape(1, rows), weight.reshape(1, rows), values)
+
+
+def extract_kernel(start_ref, weight_ref, high_ref, low_ref, out_ref):
+    rows = out_ref.shape[1]
+    slots = high_ref.shape[1]
+    chunk = 512
+    start = start_ref[...]
+    weight = weight_ref[...]
+    totals = [jnp.zeros((rows, COLS), jnp.float32) for _ in range(2)]
+    for part in range(slots // chunk):
+        slot = part * chunk + lax.broadcasted_iota(jnp.int32, (rows, chunk), 1)
+        spread = jnp.where(slot == start, weight, jnp.where(slot == start + 1, 1.0 - weight, 0.0))
+        high = spread.astype(jnp.bfloat16)
+        low = (spread - high.astype(jnp.float32)).astype(jnp.bfloat16)
+        cols = pl.ds(part * chunk, chunk)
+        for j in range(2):
+            vol_high = high_ref[j, cols, :]
+            vol_low = low_ref[j, cols, :]
+            totals[j] += jnp.dot(high, vol_high, preferred_element_type=jnp.float32)
+            totals[j] += jnp.dot(high, vol_low, preferred_element_type=jnp.float32)
+            totals[j] += jnp.dot(low, vol_high, preferred_element_type=jnp.float32)
+    for j in range(2):
+        out_ref[j] = totals[j].astype(out_ref.dtype)
+
+
+def extract_share(volume, start, weight):
+    slots = volume.shape[1] * ROWS
+    flat = volume.reshape(2, slots, COLS)
+    high = flat.astype(jnp.bfloat16)
+    low = (flat - high.astype(jnp.float32)).astype(jnp.bfloat16)
+    rows = start.size
+    return pl.pallas_call(
+        extract_kernel,
+        grid=(rows // ROWS,),
+        in_specs=[
+            pl.BlockSpec((ROWS, 1), lambda q: (q, 0)),
+            pl.BlockSpec((ROWS, 1), lambda q: (q, 0)),
+            pl.BlockSpec((2, slots, COLS), lambda q: (0, 0, 0)),
+            pl.BlockSpec((2, slots, COLS), lambda q: (0, 0, 0)),
+        ],
+        out_specs=pl.BlockSpec((2, ROWS, COLS), lambda q: (0, q, 0)),
+        out_shape=jax.ShapeDtypeStruct((2, rows, COLS), jnp.bfloat16),
+        compiler_params=pltpu.CompilerParams(vmem_limit_bytes=48 * 1024 * 1024),
+        cost_estimate=pl.CostEstimate(
+            flops=12 * rows * slots * COLS,
+            bytes_accessed=2 * 2 * slots * COLS * 2 + 2 * rows * COLS * 2,
+            transcendentals=0,
+        ),
+    )(start.reshape(rows, 1), weight.reshape(rows, 1), high, low)
 
 
 def body(
@@ -170,8 +219,12 @@
     plane_share = lax.dynamic_slice_in_dim(row_plane, first, share, 0)
     line_share = lax.dynamic_slice_in_dim(row_line, first, share, 0)
     weight_share = lax.dynamic_slice_in_dim(row_weight, first, share, 0)
-    masked = extract_rows(volume, plane_share, line_share, weight_share, slab_id)
-    own_rows = scatter_sum(masked.astype(jnp.bfloat16), "vol", 2)
+    planes_here = volume.shape[1]
+    local_plane = plane_share - slab_id * planes_here
+    in_slab = (local_plane >= 0) & (local_plane < planes_here)
+    start = jnp.where(in_slab, local_plane * ROWS + line_share, -2)
+    masked = extract_share(volume, start.reshape(-1), weight_share.reshape(-1))
+    own_rows = scatter_sum(masked.reshape(2, share, ROWS, COLS), "vol", 2)
     slices = gather_all(own_rows, "img", 1)
     cosine, sine = shift_phases(row_freq, col_freq, TRANS)
     shifted, power = make_references(slices, cosine, sine)
@@ -192,7 +245,6 @@
         jnp.where(pick[:, None, :, :], listed[:, :, :, None], jnp.zeros((), jnp.bfloat16)),
         axis=2,
     )
-    planes_here = volume.shape[1]
     y_part = jnp.einsum("btk,jbrc->tkrjc", weights, weighted, preferred_element_type=jnp.float32)
     d_part = jnp.einsum("btk,brc->tkrc", weights, squared, preferred_element_type=jnp.float32)
     num_re = jnp.sum(
@@ -204,9 +256,6 @@
     partial_value = scatter_sum(
         jnp.stack([num_re, num_im, jnp.sum(d_part, axis=0)], axis=2), "img", 0
     )
-    local_plane = plane_share - slab_id * planes_here
-    in_slab = (local_plane >= 0) & (local_plane < planes_here)
-    start = jnp.where(in_slab, local_plane * ROWS + line_share, -2)
     piece = gather_all(partial_value.astype(jnp.bfloat16), "vol", 1)
     inserted = insert_rows(
         piece.reshape(share * ROWS, 3 * COLS), start.reshape(-1), weight_share.reshape(-1), planes_here

time: 275 us -> 248 us (0.902); the launches traced: 270 us -> 247 us
  blocking collectives: 62.2 us -> 102 us
  waiting for transfers between devices: 75 us -> 38.1 us
  local copies, waits for them, and re-layouts: 51 us -> 17.3 us
  Pallas kernels: 9.99 us -> 25.7 us
  starting transfers between devices: 35.4 us -> 30.4 us
  other arithmetic: 22.7 us -> 19.5 us
    all_to_all x0 -> x1, blocking collectives: none -> 39.5 us  [gather_all(): lax.all_to_all(copies, axis_name, 0, 0, tiled=True)]
    all_to_all x3 -> x2, waiting for transfers between devices: 51.8 us -> 14.9 us  [gather_all(): lax.all_to_all(copies, axis_name, 0, 0, tiled=True)]
    gather x2 -> x0, local copies, waits for them, and re-layouts: 28.8 us -> none  [the longest x1 14.4 us: extract_rows(): upper = jnp.take(flat, line_index + 1, axis=1)]
    pallas_call x0 -> x1, Pallas kernels: none -> 15.7 us  [extract_share(): pl.pallas_call(extract_kernel, grid=(rows // ROWS,), in_specs=[pl.BlockSp...]
    all_to_all x3 -> x2, starting transfers between devices: 18 us -> 13.3 us  [gather_all(): lax.all_to_all(copies, axis_name, 0, 0, tiled=True)]
    unnamed x24 -> x28, local copies, waits for them, and re-layouts: 7.57 us -> 5.21 us
    another operation x2 -> x3, local copies, waits for them, and re-layouts: 5.56 us -> 6.84 us  [scatter_sum(): x.reshape(shape[:dim] + (count, shape[dim] // count) + shape[dim + 1:])]
  transfers between devices with their start and end apart: 5 -> 4, of which waited for: 5 -> 4; matrix products, arithmetic and copies ran while one was open for 4% -> 4% of each run, Pallas kernels for 0% -> 0%
where the time goes in v5:
time: 248 us; the launch traced here: 247 us
  blocking collectives  102 us (41%)
  waiting for transfers between devices  38.1 us (15%)
  starting transfers between devices  30.4 us (12%)
  Pallas kernels  25.7 us (10%)
  other arithmetic  19.5 us (8%)
  local copies, waits for them, and re-layouts  17.3 us (7%)
  matrix products  13.5 us (5%)
    all_to_all x2, blocking collectives, scatter_sum(): received = lax.all_to_all(split, axis_name, dim, dim, tiled=True)  62.4 us
    all_to_all x1, blocking collectives, gather_all(): lax.all_to_all(copies, axis_name, 0, 0, tiled=True)  39.5 us
    all_to_all x2, waiting for transfers between devices, scatter_sum(): received = lax.all_to_all(split, axis_name, dim, dim, tiled=True)  23.2 us
    all_to_all x2, starting transfers between devices, scatter_sum(): received = lax.all_to_all(split, axis_name, dim, dim, tiled=True)  17.1 us
    pallas_call x1, Pallas kernels, extract_share(): pl.pallas_call(extract_kernel, grid=(rows // ROWS,), in_specs=[pl.BlockSp...  15.7 us
    all_to_all x2, waiting for transfers between devices, gather_all(): lax.all_to_all(copies, axis_name, 0, 0, tiled=True)  14.9 us
    all_to_all x2, starting transfers between devices, gather_all(): lax.all_to_all(copies, axis_name, 0, 0, tiled=True)  13.3 us
    pallas_call x1, Pallas kernels, insert_rows(): pl.pallas_call(insert_kernel, grid=(planes_here,), in_specs=[pl.BlockSpec...  9.99 us
  transfers between devices with their start and end apart: 4, of which 4 were waited for; matrix products, arithmetic and copies ran while one was open for 4% of the time, Pallas kernels for 0%

profile of v5, /device:TPU:1, one launch (start us, length us, event | category | flops | bytes accessed | tf_op | source)
XLA Modules:
  0.0 246.9 jit_solution(11087685969099117278)
XLA Ops:
  1.6 1.9 fusion
  3.4 15.7 %shard_map.100 = bf16[2,2048,128]{2,1,0:T(8,128)(2,1)S(1)} custom-call(s32[2048,1]{1,0:T(8,128)S(1)} %bitcast.138, f32[2048,1]{1,0:T(8,128)S(1)} %bitcast.139, bf16[2,2048,128]{2,1,0:T(8,128)(2,1)S(1)} %get-tuple-element.8.high_ref, bf16[2,2048,128]{2,1,0:T(8,128)(2,1)S(1)} %get-tuple-element.7.low_ref), custom_call_target="tpu_custom_call" | custom-call | flops 6442450944 | bytes 3145728 | tf_op jit(solution)/shard_map/pallas_call | solution.py:178
  19.1 1.3 copy.106
  20.4 12.3 %all-to-all-start = ((bf16[2,8,32,8,128]{4,3,1,0,2:T(8,128)(2,1)}), bf16[2,8,32,8,128]{4,3,1,0,2:T(8,128)(2,1)}, u32[]{:S(2)}, u32[]{:S(2)}) async-start(bf16[2,8,32,8,128]{4,3,1,0,2:T(8,128)(2,1)} %copy.106), calls=%async_computation | async-start | bytes 2097152 | tf_op jit(solution)/shard_map/all_to_all | solution.py:97
  32.8 5.7 %fusion.6 = f32[384,8,128]{2,0,1:T(8,128)S(1)} fusion(f32[8,128]{1,0:T(8,128)S(1)} %copy-done.7, f32[8,128]{1,0:T(8,128)S(1)} %broadcast_add_fusion, f32[384]{0:T(512)S(1)} %copy-done.8), kind=kLoop, calls=%fused_computation.13 | loop fusion | flops 2359296 | bytes 1582592 | tf_op jit(solution)/shard_map/mul | solution.py:232
  40.0 1.5 multiply_convert_fusion
  41.4 1.5 fusion.48
  42.9 14.4 %all-to-all-done = bf16[2,8,32,8,128]{4,3,1,0,2:T(8,128)(2,1)} async-done(((bf16[2,8,32,8,128]{4,3,1,0,2:T(8,128)(2,1)}), bf16[2,8,32,8,128]{4,3,1,0,2:T(8,128)(2,1)}, u32[]{:S(2)}, u32[]{:S(2)}) %all-to-all-start) | async-done | bytes 1048608 | tf_op jit(solution)/shard_map/all_to_all | solution.py:97
  57.3 1.4 reduce_sum.96
  59.5 9.3 %all-to-all-start.1 = ((bf16[8,2,8,8,128]{4,2,3,1,0:T(8,128)(2,1)}), bf16[8,2,8,8,128]{4,2,3,1,0:T(8,128)(2,1)S(1)}, u32[]{:S(2)}, u32[]{:S(2)}) async-start(bf16[8,2,8,8,128]{4,2,3,1,0:T(8,128)(2,1)} %broadcast_in_dim.68), calls=%async_computation.1 | async-start | bytes 524288 | tf_op jit(solution)/shard_map/all_to_all | solution.py:104
  68.8 6.4 %all-to-all-done.1 = bf16[8,2,8,8,128]{4,2,3,1,0:T(8,128)(2,1)S(1)} async-done(((bf16[8,2,8,8,128]{4,2,3,1,0:T(8,128)(2,1)}), bf16[8,2,8,8,128]{4,2,3,1,0:T(8,128)(2,1)S(1)}, u32[]{:S(2)}, u32[]{:S(2)}) %all-to-all-start.1) | async-done | bytes 262176 | tf_op jit(solution)/shard_map/all_to_all | solution.py:104
  75.6 6.0 %fusion.19 = f32[384,64]{0,1:T(8,128)S(1)} fusion(f32[8,128]{1,0:T(8,128)S(1)} %copy-done.7, f32[8,128]{1,0:T(8,128)S(1)} %broadcast_add_fusion, f32[384]{0:T(512)S(1)} %copy-done.8, bf16[64,8,128]{2,1,0:T(8,128)(2,1)S(1)} %add_convert_fusion.1), kind=kOutput, calls=%fused_computation.25 | convolution fusion | flops 53108736 | bytes 239104 | tf_op jit(solution)/shard_map/brc,krc->bk/dot_general | solution.py:235
  81.9 1.1 copy-done.3
  86.0 4.8 %all-to-all-start.2 = ((f32[32,1,384]{2,1,0:T(1,128)}), f32[32,1,384]{2,1,0:T(1,128)S(1)}, u32[]{:S(2)}, u32[]{:S(2)}) async-start(f32[32,1,384]{2,1,0:T(1,128)} %reshape.279), calls=%async_computation.2 | async-start | bytes 98304 | tf_op jit(solution)/shard_map/all_to_all | solution.py:97
  90.8 8.8 %all-to-all-done.2 = f32[32,1,384]{2,1,0:T(1,128)S(1)} async-done(((f32[32,1,384]{2,1,0:T(1,128)}), f32[32,1,384]{2,1,0:T(1,128)S(1)}, u32[]{:S(2)}, u32[]{:S(2)}) %all-to-all-start.2) | async-done | bytes 49184 | tf_op jit(solution)/shard_map/all_to_all | solution.py:97
  102.6 4.1 %all-to-all-start.3 = ((f32[32,1,384]{2,1,0:T(1,128)}), f32[32,1,384]{2,1,0:T(1,128)S(1)}, u32[]{:S(2)}, u32[]{:S(2)}) async-start(f32[32,1,384]{2,1,0:T(1,128)} %reshape.281), calls=%async_computation.3 | async-start | bytes 98304 | tf_op jit(solution)/shard_map/all_to_all | solution.py:104
  106.7 8.5 %all-to-all-done.3 = f32[32,1,384]{2,1,0:T(1,128)S(1)} async-done(((f32[32,1,384]{2,1,0:T(1,128)}), f32[32,1,384]{2,1,0:T(1,128)S(1)}, u32[]{:S(2)}, u32[]{:S(2)}) %all-to-all-start.3) | async-done | bytes 49184 | tf_op jit(solution)/shard_map/all_to_all | solution.py:104
  118.1 6.0 %convolution_reduce_fusion = f32[64,8,128]{2,0,1:T(8,128)S(1)} fusion(f32[8,128]{1,0:T(8,128)S(1)} %copy-done.7, f32[8,128]{1,0:T(8,128)S(1)} %broadcast_add_fusion, f32[384]{0:T(512)S(1)} %copy-done.8, bf16[384,4,64]{0,2,1:T(8,128)(2,1)S(1)} %select_reduce_fusion.1), kind=kOutput, calls=%fused_computation.21 | convolution fusion | flops 204275712 | bytes 468480 | tf_op jit(solution)/shard_map/btk,brc->tkrc/dot_general | solution.py:249
  125.8 18.2 %all_to_all.35 = f32[8,8,8,3,128]{4,2,1,3,0:T(8,128)S(1)} all-to-all(f32[8,8,8,3,128]{4,2,1,3,0:T(8,128)S(1)} %pad_maximum_fusion), channel_id=1, replica_groups=mesh['img'=8,'vol'=32] {'img'}, dimensions={0} | all-to-all | bytes 1572864 | tf_op jit(solution)/shard_map/all_to_all | solution.py:97
  144.5 39.5 %all_to_all.36 = bf16[32,8,8,3,128]{4,2,3,1,0:T(8,128)(2,1)S(1)} all-to-all(bf16[32,8,8,3,128]{4,2,3,1,0:T(8,128)(2,1)S(1)} %broadcast_in_dim.86), channel_id=1, replica_groups=mesh['img'=8,'vol'=32] {'vol'}, dimensions={0} | all-to-all | bytes 3145728 | tf_op jit(solution)/shard_map/all_to_all | solution.py:104
  184.3 10.0 %shard_map.101 = f32[2048,384]{1,0:T(8,128)S(1)} custom-call(s32[1,2048]{1,0:T(1,128)S(1)} %bitcast.142, f32[1,2048]{1,0:T(1,128)S(1)} %bitcast.144, bf16[2048,384]{1,0:T(8,128)(2,1)S(1)} %bitcast.137), custom_call_target="tpu_custom_call" | custom-call | flops 6442450944 | bytes 4718592 | tf_op jit(solution)/shard_map/pallas_call | solution.py:130
  194.3 3.0 %reshape_reshape.27 = f32[8,8,32,3,128]{4,3,2,1,0:T(4,128)} reshape(f32[2048,384]{1,0:T(8,128)S(1)} %shard_map.101) | data formatting | bytes 6291456 | tf_op jit(solution)/shard_map/reshape;reshape | solution.py:96
  197.3 2.6 %copy.123 = f32[8,8,32,3,128]{4,2,3,0,1:T(8,128)S(1)} copy(f32[8,8,32,3,128]{4,3,2,1,0:T(4,128)} %reshape_reshape.27) | data formatting | bytes 6291456 | tf_op jit(solution)/shard_map/reshape;reshape | solution.py:96
  199.8 44.2 %all_to_all.37 = f32[8,8,32,3,128]{4,2,3,0,1:T(8,128)S(1)} all-to-all(f32[8,8,32,3,128]{4,2,3,0,1:T(8,128)S(1)} %copy.123), channel_id=1, replica_groups=mesh['img'=8,'vol'=32] {'img'}, dimensions={1} | all-to-all | bytes 6291456 | tf_op jit(solution)/shard_map/all_to_all | solution.py:97
  (81 shorter events, 18.4 us)
Async XLA Ops:
  0.0 1.1 copy-start
  20.4 12.4 %copy-start.7 = (f32[8,128]{1,0:T(8,128)S(1)}, f32[8,128]{1,0:T(8,128)}, u32[]{:S(2)}) copy-start(f32[8,128]{1,0:T(8,128)} %param.14) | copy-start | bytes 12292
  20.4 12.4 %copy-start.8 = (f32[384]{0:T(512)S(1)}, f32[384]{0:T(512)}, u32[]{:S(2)}) copy-start(f32[384]{0:T(512)} %param.11) | copy-start | bytes 4612
  20.4 36.9 %all-to-all-start = ((bf16[2,8,32,8,128]{4,3,1,0,2:T(8,128)(2,1)}), bf16[2,8,32,8,128]{4,3,1,0,2:T(8,128)(2,1)}, u32[]{:S(2)}, u32[]{:S(2)}) async-start(bf16[2,8,32,8,128]{4,3,1,0,2:T(8,128)(2,1)} %copy.106), calls=%async_computation | async-start | bytes 2097152 | tf_op jit(solution)/shard_map/all_to_all | solution.py:97
  38.6 0.9 copy-start.6
  38.6 1.4 copy-start.1
  42.9 25.8 %copy-start.5 = (s32[384,8]{0,1:T(8,128)S(1)}, s32[384,8]{0,1:T(8,128)}, u32[]{:S(2)}) copy-start(s32[384,8]{0,1:T(8,128)} %param.12) | copy-start | bytes 36868
  59.5 15.8 %all-to-all-start.1 = ((bf16[8,2,8,8,128]{4,2,3,1,0:T(8,128)(2,1)}), bf16[8,2,8,8,128]{4,2,3,1,0:T(8,128)(2,1)S(1)}, u32[]{:S(2)}, u32[]{:S(2)}) async-start(bf16[8,2,8,8,128]{4,2,3,1,0:T(8,128)(2,1)} %broadcast_in_dim.68), calls=%async_computation.1 | async-start | bytes 524288 | tf_op jit(solution)/shard_map/all_to_all | solution.py:104
  81.6 1.4 copy-start.3
  86.0 13.6 %all-to-all-start.2 = ((f32[32,1,384]{2,1,0:T(1,128)}), f32[32,1,384]{2,1,0:T(1,128)S(1)}, u32[]{:S(2)}, u32[]{:S(2)}) async-start(f32[32,1,384]{2,1,0:T(1,128)} %reshape.279), calls=%async_computation.2 | async-start | bytes 98304 | tf_op jit(solution)/shard_map/all_to_all | solution.py:97
  102.6 12.7 %all-to-all-start.3 = ((f32[32,1,384]{2,1,0:T(1,128)}), f32[32,1,384]{2,1,0:T(1,128)S(1)}, u32[]{:S(2)}, u32[]{:S(2)}) async-start(f32[32,1,384]{2,1,0:T(1,128)} %reshape.281), calls=%async_computation.3 | async-start | bytes 98304 | tf_op jit(solution)/shard_map/all_to_all | solution.py:104
  118.1 6.0 %copy-start.2 = (bf16[2,384,8,128,1]{3,2,1,0,4:T(8,128)(2,1)S(1)}, bf16[2,384,8,128,1]{3,2,1,0,4:T(8,128)(2,1)}, u32[]{:S(2)}) copy-start(bf16[2,384,8,128,1]{3,2,1,0,4:T(8,128)(2,1)} %fusion.48) | copy-start | bytes 4718596
  244.0 1.1 copy-start.4
